TPU v7x, 256 devices: a whole 4x4x8 slice. The times are simulated.
256 devices in a mesh: row: 8 (over z_hi, core), col: 32 (over y, x, z_lo).
Axes of the slice: x: 4, y: 4, z: 8 (z_hi: 4, z_lo: 2; z = z_hi * 2 + z_lo), core: 2. Of those that a mesh axis runs over, the one named last changes fastest.
Arguments:
- pair: bfloat16 [1536, 1536, 128], P('row', 'col'), may hold values from -6 to 6
- seq: bfloat16 [1536, 1024], P(None, 'col'), may hold values from -6 to 6
- w_hidden: bfloat16 [128, 512], replicated, may hold values from -0.5 to 0.5
- w_back: bfloat16 [512, 128], replicated, may hold values from -0.25 to 0.25
- w_bias: bfloat16 [128, 32], replicated, may hold values from -0.5 to 0.5
- w_query: bfloat16 [1024, 1024], replicated, may hold values from -10 to 10
- w_key: bfloat16 [1024, 1024], replicated, may hold values from -0.1875 to 0.1875
- w_value: bfloat16 [1024, 1024], replicated, may hold values from -0.1875 to 0.1875
- w_out: bfloat16 [1024, 1024], replicated, may hold values from -0.1875 to 0.1875
- w_project: bfloat16 [1024, 128], replicated, may hold values from -0.1875 to 0.1875
- w_pair: bfloat16 [128, 128], replicated, may hold values from -0.5 to 0.5
Outputs:
- pair_out: bfloat16 [1536, 1536, 128], P('row', 'col')
- seq_new: bfloat16 [1536, 1024], P('row', 'col')
All inputs are finite; a program needn't handle non-finite values.
Results may differ from a plain program's by a relative error of at most 0.013.
The roundings to bfloat16 on the way count: a program that leaves them out, or rounds other values in their place, can miss the bound.
Values may be sent and summed in bfloat16 or wider, within the bound.
A program may use at most 128 MiB of HBM per device.

v0:
```python
import jax
import jax.numpy as jnp
from jax import lax
from jax.sharding import PartitionSpec as P

HEADS = 32


eps_norm = 1e-05


def joined_along(tiles, dim):
    dims = list(tiles.shape[1:])
    dims[dim] *= tiles.shape[0]
    return jnp.moveaxis(tiles, 0, dim).reshape(dims)


def sent_to_all(value, axis):
    peers = lax.axis_size(axis)
    return lax.all_to_all(
        jnp.broadcast_to(value[None], (peers, *value.shape)), axis, 0, 0, tiled=True
    )


def gather_directly(value, axis, dim):
    return joined_along(sent_to_all(value, axis), dim)


def taken_together(value, axis):
    return sent_to_all(value, axis).max(axis=0)


def in_blocks(value, dim, peers):
    before, after = (value.shape[:dim], value.shape[dim + 1 :])
    return jnp.moveaxis(value.reshape(*before, peers, -1, *after), dim, 0)


def summed_on_arrival(value, axis, dim):
    peers = lax.axis_size(axis)
    tiles = lax.all_to_all(in_blocks(value, dim, peers), axis, 0, 0, tiled=True)
    return jnp.sum(tiles.astype(jnp.float32), axis=0)


def broadcast(value, axis, root):
    return lax.dynamic_index_in_dim(lax.all_gather(value, axis), root, 0, keepdims=False)


def layer_norm(values_in):
    row_mean = jnp.mean(values_in, axis=-1, keepdims=True)
    centred = values_in - row_mean
    row_var = jnp.mean(centred * centred, axis=-1, keepdims=True)
    return centred * lax.rsqrt(row_var + eps_norm)


def local(pair, seq, w_hidden, w_back, w_bias, w_query, w_key, w_value, w_out, w_project, w_pair):
    f32 = jnp.float32
    bf16 = jnp.bfloat16
    highest = lax.Precision.HIGHEST
    row_count, col_count, chans = pair.shape
    feat_width = w_query.shape[0]
    head_dim = feat_width // HEADS
    half = chans // 2
    row_index = lax.axis_index("row")
    col_index = lax.axis_index("col")
    slab_width = feat_width // lax.axis_size("col")
    own_rows = lax.dynamic_slice_in_dim(seq, row_index * row_count, row_count, 0)
    seq_rows = gather_directly(own_rows, "col", 1)
    key_rows = lax.all_to_all(seq, "col", split_axis=0, concat_axis=1, tiled=True)
    normed = layer_norm(pair.astype(f32)).astype(bf16).reshape(-1, chans)
    hidden = jax.nn.relu(jnp.dot(normed, w_hidden, preferred_element_type=f32)).astype(bf16)
    pair_mid = (
        pair.astype(f32)
        + jnp.dot(hidden, w_back, preferred_element_type=f32).reshape(row_count, col_count, chans)
    ).astype(bf16)
    mid_norm = layer_norm(pair_mid.astype(f32)).astype(bf16).reshape(-1, chans)
    pair_bias = (
        jnp.dot(mid_norm, w_bias, preferred_element_type=f32)
        .reshape(row_count, col_count, HEADS)
        .transpose(2, 0, 1)
    )
    queries = jnp.dot(
        layer_norm(seq_rows.astype(f32)).astype(bf16), w_query, preferred_element_type=f32
    ).astype(bf16)
    key_norm = layer_norm(key_rows.astype(f32)).astype(bf16)
    keys_proj = jnp.dot(key_norm, w_key, preferred_element_type=f32).astype(bf16)
    values_proj = jnp.dot(key_norm, w_value, preferred_element_type=f32).astype(bf16)
    scores = (
        jnp.einsum(
            "ihd,jhd->hij",
            queries.reshape(row_count, HEADS, head_dim),
            keys_proj.reshape(col_count, HEADS, head_dim),
            preferred_element_type=f32,
        )
        * head_dim ** (-0.5)
        + pair_bias
    )
    values_f = values_proj.astype(f32).reshape(col_count, HEADS, head_dim)
    row_top = jnp.max(scores, axis=2)
    row_top = taken_together(row_top, "col")
    weights = jnp.exp(scores - row_top[:, :, None])
    denom_sum = jnp.sum(weights, axis=2)
    weighted = jnp.einsum("hij,jhd->ihd", weights, values_f, precision=highest).reshape(
        row_count, feat_width
    )
    part_weighted, part_denom = (
        summed_on_arrival(weighted.astype(jnp.bfloat16), "col", 1),
        summed_on_arrival(denom_sum.T.astype(jnp.bfloat16), "col", 1),
    )
    attended = (part_weighted / jnp.repeat(part_denom, head_dim, axis=1)).astype(bf16)
    out_slab = lax.dynamic_slice_in_dim(w_out, col_index * slab_width, slab_width, 0)
    update = summed_on_arrival(
        jnp.einsum("pc,rp->cr", out_slab, attended, preferred_element_type=f32).astype(
            jnp.bfloat16
        ),
        "col",
        0,
    )
    seq_out = (own_rows.astype(f32) + update.T).astype(bf16)
    seq_next = gather_directly(seq_out, "col", 1)
    projected = jnp.dot(
        layer_norm(seq_next.astype(f32)).astype(bf16), w_project, preferred_element_type=f32
    ).astype(bf16)
    root_row = col_index * col_count // row_count
    offset = col_index * col_count - root_row * row_count
    own_right = lax.dynamic_slice_in_dim(projected[:, half:], offset, col_count, 0)
    right_proj = broadcast(own_right, "row", root_row).astype(f32)
    left_proj = projected[:, :half].astype(f32)
    product = left_proj[:, None, :] * right_proj[None, :, :]
    difference = left_proj[:, None, :] - right_proj[None, :, :]
    feature = jnp.concatenate([product, difference], axis=-1).astype(bf16).reshape(-1, chans)
    pair_out = (
        pair_mid.astype(f32)
        + jnp.dot(feature, w_pair, preferred_element_type=f32).reshape(row_count, col_count, chans)
    ).astype(bf16)
    return (pair_out, seq_out)


def solution(mesh):
    return jax.shard_map(
        local,
        mesh=mesh,
        in_specs=(
            P("row", "col", None),
            P(None, "col"),
            P(),
            P(),
            P(),
            P(),
            P(),
            P(),
            P(),
            P(),
            P(),
        ),
        out_specs=(P("row", "col", None), P("row", "col")),
        check_vma=False,
    )
```

profile of v0, /device:TPU:1, one launch (start us, length us, event | category | flops | bytes accessed | tf_op | source)
XLA Modules:
  0.0 180.7 jit_solution(7149492692061751664)
XLA Ops:
  0.6 0.0 copy-start
  0.6 1.3 all_to_all.29
  2.0 0.1 copy.57
  2.1 1.0 reshape.156
  3.1 9.2 %all-to-all-start.1 = ((bf16[32,2,768]{2,1,0:T(2,128)(2,1)}), bf16[32,2,768]{2,1,0:T(2,128)(2,1)S(1)}, u32[]{:S(2)}, u32[]{:S(2)}) async-start(bf16[32,2,768]{2,1,0:T(2,128)(2,1)} %reshape.156), calls=%async_computation.1 | async-start | bytes 196608 | tf_op jit(solution)/shard_map/all_to_all | solution.py:68
  12.3 0.0 copy-start.1
  12.3 3.1 %convert_reduce_fusion.1 = f32[192,48]{1,0:T(8,128)S(1)} fusion(bf16[192,48,128]{2,1,0:T(8,128)(2,1)} %param.11), kind=kLoop, calls=%fused_computation.6 | loop fusion | flops 2350080 | bytes 2396160 | tf_op jit(solution)/shard_map/reduce_sum | solution.py:49
  15.4 2.7 %fusion.6 = f32[192,48]{1,0:T(8,128)S(1)} fusion(bf16[192,48,128]{2,1,0:T(8,128)(2,1)S(1)} %copy-done.1, f32[192,48]{1,0:T(8,128)S(1)} %broadcast_multiply_fusion.1), kind=kLoop, calls=%fused_computation.13 | loop fusion | flops 4709376 | bytes 2433024 | tf_op jit(solution)/shard_map/reduce_sum | solution.py:51
  18.2 0.0 copy-start.9
  18.3 4.2 %fusion.7 = bf16[192,48,128]{2,1,0:T(8,128)(2,1)} fusion(bf16[192,48,128]{2,1,0:T(8,128)(2,1)S(1)} %copy-done.1, f32[192,48]{1,0:T(8,128)S(1)} %add_rsqrt_fusion.1, f32[192,48]{1,0:T(8,128)S(1)} %broadcast_multiply_fusion.1), kind=kLoop, calls=%fused_computation.14 | loop fusion | flops 4718592 | bytes 4792320 | tf_op jit(solution)/shard_map/convert_element_type | solution.py:69
  22.4 8.8 %fusion.10 = f32[9216,128]{1,0:T(8,128)} fusion(bf16[512,128]{1,0:T(8,128)(2,1)S(1)} %copy-done.9, bf16[9216,128]{1,0:T(8,128)(2,1)} %bitcast.70, bf16[128,512]{1,0:T(8,128)(2,1)S(1)} %copy-done.10), kind=kOutput, calls=%fused_computation.19 | convolution fusion | flops 2425356288 | bytes 7340032 | tf_op jit(solution)/shard_map/dot_general | solution.py:73
  31.3 4.4 %convert_reduce_fusion = (f32[192,48]{1,0:T(8,128)S(1)}, bf16[192,48,128]{2,1,0:T(8,128)(2,1)S(1)}) fusion(f32[192,48,128]{2,1,0:T(8,128)} %bitcast.69, bf16[192,48,128]{2,1,0:T(8,128)(2,1)} %param.11), kind=kLoop, calls=%fused_computation.3 | loop fusion | flops 5889024 | bytes 9474048 | tf_op jit(solution)/shard_map/reduce_sum | solution.py:49
  35.7 2.7 %fusion.4 = f32[192,48]{1,0:T(8,128)S(1)} fusion(bf16[192,48,128]{2,1,0:T(8,128)(2,1)S(1)} %get-tuple-element.3, f32[192,48]{1,0:T(8,128)S(1)} %broadcast_multiply_fusion), kind=kLoop, calls=%fused_computation.11 | loop fusion | flops 4709376 | bytes 2433024 | tf_op jit(solution)/shard_map/reduce_sum | solution.py:51
  38.5 5.2 %fusion.11 = f32[192,48,32]{1,2,0:T(8,128)} fusion(bf16[192,48,128]{2,1,0:T(8,128)(2,1)S(1)} %get-tuple-element.3, f32[192,48]{1,0:T(8,128)S(1)} %add_rsqrt_fusion, f32[192,48]{1,0:T(8,128)S(1)} %broadcast_multiply_fusion, bf16[128,32]{0,1:T(8,128)(2,1)S(1)} %copy-done.8), kind=kOutput, calls=%fused_computation.20 | convolution fusion | flops 80216064 | bytes 3620864 | tf_op jit(solution)/shard_map/dot_general | solution.py:77
  43.7 3.8 %copy.49 = f32[192,48,32]{0,1,2:T(8,128)} copy(f32[192,48,32]{1,2,0:T(8,128)} %fusion.11) | data formatting | bytes 2359296 | tf_op jit(solution)/shard_map/dot_general | solution.py:77
  47.5 0.8 constant_dynamic-slice_fusion.1
  48.3 0.8 broadcast_in_dim.6
  49.1 7.9 %all-to-all-start = ((bf16[32,192,32]{1,2,0:T(8,128)(2,1)}), bf16[32,192,32]{1,2,0:T(8,128)(2,1)S(1)}, u32[]{:S(2)}, u32[]{:S(2)}) async-start(bf16[32,192,32]{1,2,0:T(8,128)(2,1)} %broadcast_in_dim.6), calls=%async_computation | async-start | bytes 1048576 | tf_op jit(solution)/shard_map/all_to_all | solution.py:20
  57.0 0.2 reshape.157
  57.3 0.2 convert_reduce_fusion.6
  57.5 0.1 bitcast_convert_fusion.1
  57.5 0.9 copy.53
  58.4 0.2 multiply_reduce_fusion.2
  58.5 2.2 %convolution_convert_fusion.3 = bf16[48,1024]{1,0:T(8,128)(2,1)S(1)} fusion(bf16[1024,1024]{1,0:T(8,128)(2,1)} %param.17, f32[48,1024]{1,0:T(8,128)} %copy.53, f32[48]{0:T(128)S(1)} %add_rsqrt_fusion.4, f32[48]{0:T(128)S(1)} %broadcast_multiply_fusion.4), kind=kOutput, calls=%fused_computation.35 | convolution fusion | flops 100859904 | bytes 2392448 | tf_op jit(solution)/shard_map/dot_general | solution.py:85
  60.8 0.2 copy.54
  61.0 6.9 %all-to-all-done = bf16[32,192,32]{1,2,0:T(8,128)(2,1)S(1)} async-done(((bf16[32,192,32]{1,2,0:T(8,128)(2,1)}), bf16[32,192,32]{1,2,0:T(8,128)(2,1)S(1)}, u32[]{:S(2)}, u32[]{:S(2)}) %all-to-all-start) | async-done | bytes 393248 | tf_op jit(solution)/shard_map/all_to_all | solution.py:20
  67.9 0.2 convert_reduce_fusion.5
  68.0 0.2 multiply_reduce_fusion.1
  68.2 0.1 fusion.27
  68.4 0.6 convolution_convert_fusion.1
  69.0 0.2 copy.45
  69.2 3.0 %fusion.38 = (f32[32,192]{1,0:T(8,128)S(1)}, f32[32,192,48]{1,2,0:T(8,128)}) fusion(f32[192,48,32]{0,1,2:T(8,128)} %copy.49, bf16[192,32,32]{0,2,1:T(8,128)(2,1)S(1)} %bitcast.71, bf16[48,32,32]{0,2,1:T(8,128)(2,1)S(1)} %bitcast.76), kind=kOutput, calls=%fused_computation.79 | convolution fusion | flops 19752960 | bytes 2875392 | tf_op jit(solution)/shard_map/ihd,jhd->hij/dot_general | solution.py:88
  72.2 1.1 broadcast_in_dim.7
  73.3 3.9 %all-to-all-start.2 = ((f32[32,32,192]{2,1,0:T(8,128)}), f32[32,32,192]{2,1,0:T(8,128)S(1)}, u32[]{:S(2)}, u32[]{:S(2)}) async-start(f32[32,32,192]{2,1,0:T(8,128)} %broadcast_in_dim.7), calls=%async_computation.2 | async-start | bytes 2097152 | tf_op jit(solution)/shard_map/all_to_all | solution.py:20
  77.3 2.1 %convolution_convert_fusion.2 = bf16[48,1024]{1,0:T(8,128)(2,1)S(1)} fusion(bf16[1024,1024]{1,0:T(8,128)(2,1)} %param.18, f32[48,1024]{1,0:T(8,128)S(1)} %copy-done.4, f32[48]{0:T(128)S(1)} %add_rsqrt_fusion.4, f32[48]{0:T(128)S(1)} %broadcast_multiply_fusion.4), kind=kOutput, calls=%fused_computation.34 | convolution fusion | flops 100859904 | bytes 2392448 | tf_op jit(solution)/shard_map/dot_general | solution.py:86
  79.4 0.2 copy.55
  79.6 13.3 %all-to-all-done.2 = f32[32,32,192]{2,1,0:T(8,128)S(1)} async-done(((f32[32,32,192]{2,1,0:T(8,128)}), f32[32,32,192]{2,1,0:T(8,128)S(1)}, u32[]{:S(2)}, u32[]{:S(2)}) %all-to-all-start.2) | async-done | bytes 786464 | tf_op jit(solution)/shard_map/all_to_all | solution.py:20
  92.9 0.1 reduce_max.19
  93.0 1.7 fusion.21
  94.7 0.6 copy.51
  95.4 4.6 %all-to-all-start.4 = ((bf16[32,192,1]{1,2,0:T(2,128)(2,1)}), bf16[32,192,1]{1,2,0:T(2,128)(2,1)S(1)}, u32[]{:S(2)}, u32[]{:S(2)}) async-start(bf16[32,192,1]{1,2,0:T(2,128)(2,1)} %copy.51), calls=%async_computation.4 | async-start | bytes 65536 | tf_op jit(solution)/shard_map/all_to_all | solution.py:40
  99.9 3.2 %fusion.23 = bf16[32,192,32]{1,2,0:T(8,128)(2,1)} fusion(bf16[48,32,32]{0,2,1:T(8,128)(2,1)S(1)} %bitcast.74, f32[32,192,48]{1,2,0:T(8,128)} %get-tuple-element.9, f32[32,192]{1,0:T(8,128)S(1)} %reduce_max.19), kind=kOutput, calls=%fused_computation.31 | convolution fusion | flops 113737728 | bytes 1695744 | tf_op jit(solution)/shard_map/hij,jhd->ihd/dot_general | solution.py:102
  103.1 4.0 %all-to-all-done.4 = bf16[32,192,1]{1,2,0:T(2,128)(2,1)S(1)} async-done(((bf16[32,192,1]{1,2,0:T(2,128)(2,1)}), bf16[32,192,1]{1,2,0:T(2,128)(2,1)S(1)}, u32[]{:S(2)}, u32[]{:S(2)}) %all-to-all-start.4) | async-done | bytes 12320 | tf_op jit(solution)/shard_map/all_to_all | solution.py:40
  107.1 3.9 %all-to-all-start.3 = ((bf16[32,192,32]{1,2,0:T(8,128)(2,1)}), bf16[32,192,32]{1,2,0:T(8,128)(2,1)S(1)}, u32[]{:S(2)}, u32[]{:S(2)}) async-start(bf16[32,192,32]{1,2,0:T(8,128)(2,1)} %fusion.23), calls=%async_computation.3 | async-start | bytes 1048576 | tf_op jit(solution)/shard_map/all_to_all | solution.py:40
  111.0 0.1 convert_reduce_fusion.7
  111.0 9.7 %all-to-all-done.3 = bf16[32,192,32]{1,2,0:T(8,128)(2,1)S(1)} async-done(((bf16[32,192,32]{1,2,0:T(8,128)(2,1)}), bf16[32,192,32]{1,2,0:T(8,128)(2,1)S(1)}, u32[]{:S(2)}, u32[]{:S(2)}) %all-to-all-start.3) | async-done | bytes 393248 | tf_op jit(solution)/shard_map/all_to_all | solution.py:40
  120.7 0.1 convert_reduce_fusion.3
  120.8 1.1 convolution_convert_fusion
  121.9 0.2 copy.52
  122.1 13.3 %all_to_all.43 = bf16[32,32,192]{2,1,0:T(8,128)(2,1)S(1)} all-to-all(bf16[32,32,192]{2,1,0:T(8,128)(2,1)S(1)} %bitcast.72), channel_id=1, replica_groups=mesh['row'=8,'col'=32] {'col'}, dimensions={0} | all-to-all | bytes 786432 | tf_op jit(solution)/shard_map/all_to_all | solution.py:40
  135.4 0.1 convert_reduce_fusion.2
  135.5 0.8 fusion.31
  136.3 0.8 broadcast_in_dim.8
  137.2 3.9 %all-to-all-start.6 = ((bf16[32,192,32]{1,2,0:T(8,128)(2,1)}), bf16[32,192,32]{1,2,0:T(8,128)(2,1)S(1)}, u32[]{:S(2)}, u32[]{:S(2)}) async-start(bf16[32,192,32]{1,2,0:T(8,128)(2,1)} %broadcast_in_dim.8), calls=%async_computation.6 | async-start | bytes 1048576 | tf_op jit(solution)/shard_map/all_to_all | solution.py:20
  141.1 9.7 %all-to-all-done.6 = bf16[32,192,32]{1,2,0:T(8,128)(2,1)S(1)} async-done(((bf16[32,192,32]{1,2,0:T(8,128)(2,1)}), bf16[32,192,32]{1,2,0:T(8,128)(2,1)S(1)}, u32[]{:S(2)}, u32[]{:S(2)}) %all-to-all-start.6) | async-done | bytes 393248 | tf_op jit(solution)/shard_map/all_to_all | solution.py:20
  150.8 0.2 convert_reduce_fusion.4
  151.0 0.2 multiply_reduce_fusion
  151.2 0.1 fusion.25
  151.3 0.3 convolution_convert_fusion.4
  151.7 0.1 slice_convert_fusion
  151.8 24.1 %all-gather = bf16[384,64]{1,0:T(8,128)(2,1)S(1)} all-gather(bf16[48,64]{1,0:T(8,128)(2,1)S(1)} %constant_dynamic-slice_fusion), channel_id=2, replica_groups=mesh['row'=8,'col'=32] {'row'}, dimensions={0}, use_global_device_ids=true | all-gather | bytes 55296 | tf_op jit(solution)/shard_map/all_gather | solution.py:45
  175.9 0.8 multiply_convert_fusion
  176.7 0.9 copy-done.3
  177.6 3.1 %fusion.9 = bf16[192,48,128]{2,1,0:T(8,128)(2,1)} fusion(bf16[192,48,128]{2,1,0:T(8,128)(2,1)S(1)} %copy-done.3, bf16[192,48,64]{2,1,0:T(8,128)(2,1)S(1)} %get-tuple-element.5, bf16[192,48,64]{2,1,0:T(8,128)(2,1)S(1)} %get-tuple-element.4, bf16[128,128]{1,0:T(8,128)(2,1)S(1)} %copy-done.7), kind=kOutput, calls=%fused_computation.16 | convolution fusion | flops 310247424 | bytes 7110656 | tf_op jit(solution)/shard_map/dot_general | solution.py:133
  (31 shorter events, 0.2 us)
Async XLA Ops:
  0.6 67.8 %copy-start = (bf16[1024,1024]{1,0:T(8,128)(2,1)S(1)}, bf16[1024,1024]{1,0:T(8,128)(2,1)}, u32[]{:S(2)}) copy-start(bf16[1024,1024]{1,0:T(8,128)(2,1)} %param.16) | copy-start | bytes 6291460
  3.1 45.2 %all-to-all-start.1 = ((bf16[32,2,768]{2,1,0:T(2,128)(2,1)}), bf16[32,2,768]{2,1,0:T(2,128)(2,1)S(1)}, u32[]{:S(2)}, u32[]{:S(2)}) async-start(bf16[32,2,768]{2,1,0:T(2,128)(2,1)} %reshape.156), calls=%async_computation.1 | async-start | bytes 196608 | tf_op jit(solution)/shard_map/all_to_all | solution.py:68
  12.3 3.1 %copy-start.1 = (bf16[192,48,128]{2,1,0:T(8,128)(2,1)S(1)}, bf16[192,48,128]{2,1,0:T(8,128)(2,1)}, u32[]{:S(2)}) copy-start(bf16[192,48,128]{2,1,0:T(8,128)(2,1)} %param.11) | copy-start | bytes 7077892
  18.2 4.2 %copy-start.9 = (bf16[512,128]{1,0:T(8,128)(2,1)S(1)}, bf16[512,128]{1,0:T(8,128)(2,1)}, u32[]{:S(2)}) copy-start(bf16[512,128]{1,0:T(8,128)(2,1)} %param.14) | copy-start | bytes 393220
  18.2 4.2 %copy-start.10 = (bf16[128,512]{1,0:T(8,128)(2,1)S(1)}, bf16[128,512]{1,0:T(8,128)(2,1)}, u32[]{:S(2)}) copy-start(bf16[128,512]{1,0:T(8,128)(2,1)} %param.13) | copy-start | bytes 393220
  35.7 8.0 %copy-start.2 = (bf16[192,48,128]{2,1,0:T(8,128)(2,1)}, bf16[192,48,128]{2,1,0:T(8,128)(2,1)S(1)}, u32[]{:S(2)}) copy-start(bf16[192,48,128]{2,1,0:T(8,128)(2,1)S(1)} %get-tuple-element.3) | copy-start | bytes 7077892
  35.7 2.8 %copy-start.8 = (bf16[128,32]{0,1:T(8,128)(2,1)S(1)}, bf16[128,32]{0,1:T(8,128)(2,1)}, u32[]{:S(2)}) copy-start(bf16[128,32]{0,1:T(8,128)(2,1)} %param.15) | copy-start | bytes 24580
  49.1 18.7 %all-to-all-start = ((bf16[32,192,32]{1,2,0:T(8,128)(2,1)}), bf16[32,192,32]{1,2,0:T(8,128)(2,1)S(1)}, u32[]{:S(2)}, u32[]{:S(2)}) async-start(bf16[32,192,32]{1,2,0:T(8,128)(2,1)} %broadcast_in_dim.6), calls=%async_computation | async-start | bytes 1048576 | tf_op jit(solution)/shard_map/all_to_all | solution.py:20
  72.2 5.0 %copy-start.4 = (f32[48,1024]{1,0:T(8,128)S(1)}, f32[48,1024]{1,0:T(8,128)}, u32[]{:S(2)}) copy-start(f32[48,1024]{1,0:T(8,128)} %copy.53) | copy-start | bytes 589828
  73.3 19.6 %all-to-all-start.2 = ((f32[32,32,192]{2,1,0:T(8,128)}), f32[32,32,192]{2,1,0:T(8,128)S(1)}, u32[]{:S(2)}, u32[]{:S(2)}) async-start(f32[32,32,192]{2,1,0:T(8,128)} %broadcast_in_dim.7), calls=%async_computation.2 | async-start | bytes 2097152 | tf_op jit(solution)/shard_map/all_to_all | solution.py:20
  95.4 11.7 %all-to-all-start.4 = ((bf16[32,192,1]{1,2,0:T(2,128)(2,1)}), bf16[32,192,1]{1,2,0:T(2,128)(2,1)S(1)}, u32[]{:S(2)}, u32[]{:S(2)}) async-start(bf16[32,192,1]{1,2,0:T(2,128)(2,1)} %copy.51), calls=%async_computation.4 | async-start | bytes 65536 | tf_op jit(solution)/shard_map/all_to_all | solution.py:40
  107.1 13.6 %all-to-all-start.3 = ((bf16[32,192,32]{1,2,0:T(8,128)(2,1)}), bf16[32,192,32]{1,2,0:T(8,128)(2,1)S(1)}, u32[]{:S(2)}, u32[]{:S(2)}) async-start(bf16[32,192,32]{1,2,0:T(8,128)(2,1)} %fusion.23), calls=%async_computation.3 | async-start | bytes 1048576 | tf_op jit(solution)/shard_map/all_to_all | solution.py:40
  135.4 15.9 %copy-start.5 = (bf16[1024,128]{1,0:T(8,128)(2,1)S(1)}, bf16[1024,128]{1,0:T(8,128)(2,1)}, u32[]{:S(2)}) copy-start(bf16[1024,128]{1,0:T(8,128)(2,1)} %param.20) | copy-start | bytes 786436
  136.3 15.4 %copy-start.6 = (bf16[192,32]{0,1:T(8,128)(2,1)}, bf16[192,32]{0,1:T(8,128)(2,1)S(1)}, u32[]{:S(2)}) copy-start(bf16[192,32]{0,1:T(8,128)(2,1)S(1)} %fusion.31) | copy-start | bytes 36868
  137.2 13.6 %all-to-all-start.6 = ((bf16[32,192,32]{1,2,0:T(8,128)(2,1)}), bf16[32,192,32]{1,2,0:T(8,128)(2,1)S(1)}, u32[]{:S(2)}, u32[]{:S(2)}) async-start(bf16[32,192,32]{1,2,0:T(8,128)(2,1)} %broadcast_in_dim.8), calls=%async_computation.6 | async-start | bytes 1048576 | tf_op jit(solution)/shard_map/all_to_all | solution.py:20
  175.9 1.7 copy-start.3
  175.9 1.7 copy-start.7
where the time goes:
time: 182 us; the launch traced here: 181 us
  waiting for transfers between devices  43.5 us (24%)
  blocking collectives  37.4 us (21%)
  starting transfers between devices  33.4 us (18%)
  matrix products  29.7 us (16%)
  other arithmetic  22.4 us (12%)
  local copies, waits for them, and re-layouts  13.3 us (7%)
    all_to_all x3, waiting for transfers between devices, sent_to_all(): lax.all_to_all(jnp.broadcast_to(value[None], (peers, *value.shape)), axis...  29.9 us
    all_gather x1, blocking collectives, broadcast(): lax.all_gather(value, axis)  24.1 us
    all_to_all x3, starting transfers between devices, sent_to_all(): lax.all_to_all(jnp.broadcast_to(value[None], (peers, *value.shape)), axis...  15.7 us
    all_to_all x2, waiting for transfers between devices, summed_on_arrival(): tiles = lax.all_to_all(in_blocks(value, dim, peers), axis, 0, 0, tiled=True)  13.6 us
    all_to_all x1, blocking collectives, summed_on_arrival(): tiles = lax.all_to_all(in_blocks(value, dim, peers), axis, 0, 0, tiled=True)  13.3 us
    all_to_all x1, starting transfers between devices, local(): lax.all_to_all(seq, 'col', split_axis=0, concat_axis=1, tiled=True)  9.21 us
    dot_general x1, matrix products, local(): jnp.dot(hidden, w_back, preferred_element_type=f32)  8.85 us
    all_to_all x2, starting transfers between devices, summed_on_arrival(): tiles = lax.all_to_all(in_blocks(value, dim, peers), axis, 0, 0, tiled=True)  8.46 us
  transfers between devices with their start and end apart: 6, of which 5 were waited for; matrix products, arithmetic and copies ran while one was open for 25% of the time, Pallas kernels for 0%

commit v1 on v0

v1 whole, which is shorter than its diff:
```python
import functools

import jax
import jax.numpy as jnp
from jax import lax
from jax.experimental import pallas as pl
from jax.experimental.pallas import tpu as pltpu
from jax.sharding import PartitionSpec as P

HEADS = 32
EPS = 1e-05
F32 = jnp.float32
BF16 = jnp.bfloat16

R_DEV, C_DEV = 8, 32
NI, NJ, C, D, PH = 192, 48, 128, 1024, 512
OWNERS, OWN = 24, 8
WL = D + 128
RC = 16
SCALE = 32 ** (-0.5)
MESH = pl.DeviceIdType.MESH


def nt(a, b):
    return lax.dot_general(a, b, (((1,), (1,)), ((), ())), preferred_element_type=F32)


def nn(a, b):
    return jnp.dot(a, b, preferred_element_type=F32)


def layer_norm(x, axis=-1):
    mean = jnp.mean(x, axis=axis, keepdims=True)
    cen = x - mean
    var = jnp.mean(cen * cen, axis=axis, keepdims=True)
    return cen * lax.rsqrt(var + EPS)


def iota(shape, dim):
    return lax.broadcasted_iota(jnp.int32, shape, dim)


def owner_of(col):
    y, x, z = col // 8, (col // 2) % 4, col % 2
    xr = jnp.where(x > y, x - 1, x)
    return (y * 3 + xr) * 2 + z, x != y, y


def col_of(y, t):
    xr, z = t // 2, t % 2
    x = jnp.where(xr >= y, xr + 1, xr)
    return (y * 4 + x) * 2 + z


def main_kernel(
    pair_h, seq_h, whid_h, wback_h, wbias_h, wq_h, wk_h, wv_h, wout_h, wproj_h,
    mid_h, left_o, right_o, seq_o,
    pair_v, mid_v, mn_v, bias_v, bmat_v, seq_v, whid_v, wback_v, wbias_v, wq_v, wk_v, wv_v, wout_v, wproj_v,
    msgs, sqk, q_v, kv_v, kbd, vbd, w_v, wmsg, wrecv, emsg, erecv, rmsg, rrecv,
    in_sem, pin_sem, mid_sem, s_send, s_recv, w_send, w_recv, e_send, e_recv, r_send, r_recv,
):
    me_r, me_c = lax.axis_index("row"), lax.axis_index("col")
    own_o, is_owner, me_y = owner_of(me_c)
    own_o = jnp.where(is_owner, own_o, 0)
    dest_c = 4 * me_r + me_y
    self_right = jnp.logical_and(is_owner, dest_c == me_c)

    barrier = pltpu.get_barrier_semaphore()

    def greet(s, _):
        pl.semaphore_signal(barrier, 1, device_id=(me_r, (me_c + s) % C_DEV), device_id_type=MESH)
        return 0

    lax.fori_loop(1, C_DEV, greet, 0)
    src_r, src_y = me_c // 4, me_c % 4

    def greet_right(t, _):
        src = col_of(src_y, t)

        @pl.when(jnp.logical_not(jnp.logical_and(src_r == me_r, src == me_c)))
        def _():
            pl.semaphore_signal(barrier, 1, device_id=(src_r, src), device_id_type=MESH)

        return 0

    lax.fori_loop(0, 6, greet_right, 0)

    def load(src, dst, k):
        cp = pltpu.make_async_copy(src, dst, in_sem.at[k])
        cp.start()
        return cp

    c_seq = load(seq_h, seq_v, 0)
    c_hid = load(whid_h, whid_v, 1)
    c_back = load(wback_h, wback_v, 2)
    c_bias = load(wbias_h, wbias_v, 3)
    n_steps = NI // RC
    pair_in = []
    for k in range(n_steps):
        rows = pl.ds(k * RC, RC)
        cp = pltpu.make_async_copy(pair_h.at[rows], pair_v.at[rows], pin_sem.at[k])
        cp.start()
        pair_in.append(cp)
    c_q = load(wq_h, wq_v, 4)
    c_k = load(wk_h, wk_v, 5)
    c_v = load(wv_h, wv_v, 6)
    c_out = load(wout_h, wout_v, 7)
    c_proj = load(wproj_h, wproj_v, 8)

    c_seq.wait()
    eye = jnp.where(iota((32, 32), 0) == iota((32, 32), 1), 1.0, 0.0).astype(BF16)
    own_rows = seq_v[pl.ds(pl.multiple_of(me_r * NI, 64), NI), :]
    first = nt(eye, own_rows[:128]).astype(BF16)
    tail = own_rows[128:]
    pad = jnp.zeros((16, 32), BF16)

    def message(s, _):
        dst = (me_c + s) % C_DEV
        keys = seq_v[pl.ds(pl.multiple_of(dst * NJ, 16), NJ), :]
        second = nt(eye, jnp.concatenate([tail, keys, pad], axis=0)).astype(BF16)
        msgs[dst, :, 0:128] = first
        msgs[dst, :, 128:256] = second
        return 0

    lax.fori_loop(0, C_DEV, message, 0)

    pl.semaphore_wait(
        barrier, C_DEV - 1 + jnp.where(is_owner, R_DEV, 0) - jnp.where(self_right, 1, 0)
    )
    my_slab = pl.ds(pl.multiple_of(me_c * 32, 32), 32)

    def send_seq(s, _):
        dst = (me_c + s) % C_DEV
        pltpu.make_async_remote_copy(
            msgs.at[dst], sqk.at[my_slab], s_send, s_recv, device_id=(me_r, dst), device_id_type=MESH
        ).start()
        return 0

    lax.fori_loop(1, C_DEV, send_seq, 0)
    pltpu.make_async_copy(msgs.at[me_c], sqk.at[my_slab], s_recv).start()

    c_bias.wait()
    spread = jnp.where(
        iota((32, 256), 0) == (iota((32, 256), 1) // 128) * 16 + iota((32, 256), 1) % 16, 1.0, 0.0
    ).astype(BF16)
    wide = nn(wbias_v[...], spread)
    slot = (iota((C, 256), 1) % 128) // 16
    for j8 in range(8):
        bmat_v[j8 * C : (j8 + 1) * C, :] = jnp.where(slot == j8, wide, 0.0).astype(BF16)

    c_hid.wait()
    c_back.wait()

    def pair_step(k, _):
        i0 = pl.multiple_of(k * RC, RC)
        rows = pl.ds(i0, RC)
        pltpu.make_async_copy(pair_h.at[rows], pair_v.at[rows], pin_sem.at[k]).wait()
        x = pair_v[rows].astype(F32).reshape(RC * NJ, C)
        hid = jnp.maximum(nn(layer_norm(x).astype(BF16), whid_v[...]), 0.0).astype(BF16)
        mid = (x + nn(hid, wback_v[...])).astype(BF16)
        mid_v[rows] = mid.reshape(RC, NJ, C)
        mn_v[...] = layer_norm(mid.astype(F32))
        blocks = []
        for jb in range(6):
            cols = []
            for j8 in range(8):
                j = jb * 8 + j8
                cols.append(
                    jnp.concatenate(
                        [mn_v[pl.ds(h * 8 * NJ + j, 8, stride=NJ), :] for h in range(RC // 8)], axis=0
                    ).astype(BF16)
                )
            blocks.append(jnp.concatenate(cols, axis=1))
        out = nn(jnp.concatenate(blocks, axis=0), bmat_v[...])
        for jb in range(6):
            for g in range(2):
                bias_v[g, jb, rows, :] = out[jb * RC : (jb + 1) * RC, g * 128 : (g + 1) * 128]
        pltpu.make_async_copy(mid_v.at[rows], mid_h.at[rows], mid_sem).start()
        return 0

    lax.fori_loop(0, n_steps, pair_step, 0)

    pltpu.make_async_copy(sqk, sqk, s_recv).wait()
    ident = jnp.where(iota((256, 256), 0) == iota((256, 256), 1), 1.0, 0.0).astype(BF16)
    normed = nt(ident, layer_norm(sqk[...].astype(F32), 0).astype(BF16)).astype(BF16)
    c_q.wait()
    q_v[...] = nn(normed[:NI], wq_v[...]).astype(BF16)
    c_k.wait()
    c_v.wait()
    kv_v[:, 0:D] = nn(normed[NI : NI + NJ], wk_v[...])
    kv_v[:, D : 2 * D] = nn(normed[NI : NI + NJ], wv_v[...])
    head_here = iota((16, 512), 0) == iota((16, 512), 1) // 32

    def spread_keys(j, _):
        dst = pl.ds(pl.multiple_of(j * 16, 16), 16)
        for g in range(2):
            krow = jnp.broadcast_to(kv_v[pl.ds(j, 1), g * 512 : (g + 1) * 512], (16, 512))
            vrow = jnp.broadcast_to(kv_v[pl.ds(j, 1), D + g * 512 : D + (g + 1) * 512], (16, 512))
            kbd[g, dst, :] = jnp.where(head_here, krow, 0.0).astype(BF16)
            vbd[g, dst, :] = jnp.where(head_here, vrow, 0.0).astype(BF16)
        return 0

    lax.fori_loop(0, NJ, spread_keys, 0)

    lane = iota((NI, 128), 1)
    parts = []
    for g in range(2):
        scores = nt(q_v[:, g * 512 : (g + 1) * 512], kbd[g])
        tiles = [scores[:, jb * 128 : (jb + 1) * 128] * SCALE + bias_v[g, jb] for jb in range(6)]
        top = functools.reduce(jnp.maximum, tiles)
        for shift in (16, 32, 64):
            top = jnp.maximum(top, pltpu.roll(top, shift, 1))
        total = None
        for jb in range(6):
            w = jnp.exp(tiles[jb] - top)
            w_v[g, :, jb * 128 : (jb + 1) * 128] = w.astype(BF16)
            total = w if total is None else total + w
        for shift in (16, 32, 64):
            total = total + pltpu.roll(total, shift, 1)
        weighted = nn(w_v[g], vbd[g])
        wmsg[:, :, g * 512 : (g + 1) * 512] = weighted.reshape(OWNERS, OWN, 512).astype(BF16)
        high = top.astype(BF16).astype(F32)
        middle = (top - high).astype(BF16).astype(F32)
        low = (top - high) - middle
        parts.append((high, middle, low, total))
    stats = jnp.zeros((NI, 128), F32)
    for p in range(4):
        for g in range(2):
            stats = jnp.where(lane // 16 == p * 2 + g, parts[g][p], stats)
    wmsg[:, :, D:WL] = stats.reshape(OWNERS, OWN, 128).astype(BF16)

    def send_rows(s, _):
        dst = (me_c + s) % C_DEV
        o, owns, _y = owner_of(dst)

        @pl.when(owns)
        def _():
            pltpu.make_async_remote_copy(
                wmsg.at[o], wrecv.at[me_c], w_send, w_recv, device_id=(me_r, dst), device_id_type=MESH
            ).start()

        return 0

    lax.fori_loop(1, C_DEV, send_rows, 0)

    @pl.when(is_owner)
    def _():
        pltpu.make_async_copy(wmsg.at[own_o], wrecv.at[me_c], w_recv).start()
        pick = jnp.where(iota((8, 256), 1) == own_o * 8 + iota((8, 256), 0), 1.0, 0.0).astype(BF16)
        resid = nt(pick, sqk[...])
        head_lane = iota((128, D), 0) == iota((128, D), 1) // 32
        expand = jnp.where(head_lane, 1.0, 0.0).astype(BF16)
        c_out.wait()
        c_proj.wait()
        pltpu.make_async_copy(wrecv, wrecv, w_recv).wait()
        st = wrecv[:, :, D:WL].astype(F32).reshape(C_DEV * OWN, 128)
        m = (st + pltpu.roll(st, 96, 1)) + pltpu.roll(st, 64, 1)
        den = pltpu.roll(st, 32, 1)
        m3 = m.reshape(C_DEV, OWN, 128)
        top = jnp.max(m3, axis=0)
        fac = jnp.where(iota((C_DEV, OWN, 128), 2) < 32, jnp.exp(jnp.minimum(m3 - top[None], 0.0)), 0.0)
        whole = jnp.sum(fac * den.reshape(C_DEV, OWN, 128), axis=0)
        whole = jnp.where(iota((OWN, 128), 1) < 32, whole, 1.0)
        fac = (fac / whole[None]).reshape(C_DEV * OWN, 128)
        high = fac.astype(BF16)
        low = (fac - high.astype(F32)).astype(BF16)
        wide = (nn(high, expand) + nn(low, expand)).reshape(C_DEV, OWN, D)
        attended = jnp.sum(wide * wrecv[:, :, 0:D].astype(F32), axis=0).astype(BF16)
        seq_new = (resid + nn(attended, wout_v[...])).astype(BF16).astype(F32)
        proj = nn(layer_norm(seq_new).astype(BF16), wproj_v[...]).astype(BF16).astype(F32)
        turned = pltpu.roll(proj, 64, 1)
        lane8 = iota((OWN, 128), 1)
        left = jnp.where(lane8 < 64, proj, turned).astype(BF16)
        right = jnp.where(lane8 < 64, turned, proj).astype(BF16)
        rmsg[...] = right
        for c in range(C_DEV):
            tile = seq_new[:, (c // 4) * 128 : (c // 4) * 128 + 128]
            if c % 4:
                tile = pltpu.roll(tile, 128 - 32 * (c % 4), 1)
            emsg[c, 0] = left
            emsg[c, 1] = tile.astype(BF16)

        def send_right(r, _):
            here = jnp.logical_and(r == me_r, dest_c == me_c)

            @pl.when(jnp.logical_not(here))
            def _():
                pltpu.make_async_remote_copy(
                    rmsg, rrecv.at[own_o % 6], r_send, r_recv, device_id=(r, dest_c), device_id_type=MESH
                ).start()

            @pl.when(here)
            def _():
                pltpu.make_async_copy(rmsg, rrecv.at[own_o % 6], r_recv).start()

            return 0

        lax.fori_loop(0, R_DEV, send_right, 0)

        def send_left(s, _):
            dst = (me_c + s) % C_DEV
            pltpu.make_async_remote_copy(
                emsg.at[dst], erecv.at[own_o], e_send, e_recv, device_id=(me_r, dst), device_id_type=MESH
            ).start()
            return 0

        lax.fori_loop(1, C_DEV, send_left, 0)
        pltpu.make_async_copy(emsg.at[me_c], erecv.at[own_o], e_recv).start()

    @pl.when(jnp.logical_not(is_owner))
    def _():
        c_out.wait()
        c_proj.wait()

    pltpu.make_async_copy(mid_v, mid_h, mid_sem).wait()
    pltpu.make_async_copy(rrecv, rrecv, r_recv).wait()
    right_o[...] = rrecv[...].astype(F32).reshape(NJ, 128)
    pltpu.make_async_copy(erecv, erecv, e_recv).wait()
    left_o[...] = erecv[:, 0].astype(F32).reshape(NI, 128)
    seq_o[...] = erecv[:, 1].astype(F32).reshape(NI, 128)[:, 0:32].astype(BF16)

    pltpu.make_async_copy(msgs.at[0 : C_DEV - 1], msgs.at[0 : C_DEV - 1], s_send).wait()

    def sent_rows(s, _):
        o, owns, _y = owner_of((me_c + s) % C_DEV)

        @pl.when(owns)
        def _():
            pltpu.make_async_copy(wmsg.at[o], wmsg.at[o], w_send).wait()

        return 0

    lax.fori_loop(1, C_DEV, sent_rows, 0)

    @pl.when(is_owner)
    def _():
        pltpu.make_async_copy(emsg.at[0 : C_DEV - 1], emsg.at[0 : C_DEV - 1], e_send).wait()

        def sent_right(r, _):
            @pl.when(jnp.logical_not(jnp.logical_and(r == me_r, dest_c == me_c)))
            def _():
                pltpu.make_async_copy(rmsg, rmsg, r_send).wait()

            return 0

        lax.fori_loop(0, R_DEV, sent_right, 0)


def pair_kernel(mid_ref, left_ref, right_ref, wpair_ref, out_ref):
    n = mid_ref.shape[0]
    lane = iota((NJ, C), 1)
    right = right_ref[...]
    scale = jnp.where(lane < 64, right, 1.0)
    shift = jnp.where(lane < 64, 0.0, -right)
    left = left_ref[...].reshape(n, 1, C)
    feature = (left * scale[None] + shift[None]).astype(BF16).reshape(n * NJ, C)
    update = nn(feature, wpair_ref[...])
    mid = mid_ref[...].astype(F32).reshape(n * NJ, C)
    out_ref[...] = (mid + update).astype(BF16).reshape(n, NJ, C)


def local(pair, seq, w_hidden, w_back, w_bias, w_query, w_key, w_value, w_out, w_project, w_pair):
    hbm = pl.BlockSpec(memory_space=pl.ANY)
    vmem = pl.BlockSpec(memory_space=pltpu.VMEM)
    dma = pltpu.SemaphoreType.DMA
    mid, left, right, seq_new = pl.pallas_call(
        main_kernel,
        out_shape=(
            jax.ShapeDtypeStruct((NI, NJ, C), BF16),
            jax.ShapeDtypeStruct((NI, 128), F32),
            jax.ShapeDtypeStruct((NJ, 128), F32),
            jax.ShapeDtypeStruct((NI, 32), BF16),
        ),
        in_specs=[hbm] * 10,
        out_specs=(hbm, vmem, vmem, vmem),
        scratch_shapes=[
            pltpu.VMEM((NI, NJ, C), BF16),
            pltpu.VMEM((NI, NJ, C), BF16),
            pltpu.VMEM((RC * NJ, C), F32),
            pltpu.VMEM((2, 6, NI, 128), F32),
            pltpu.VMEM((8 * C, 256), BF16),
            pltpu.VMEM((R_DEV * NI, 32), BF16),
            pltpu.VMEM((C, PH), BF16),
            pltpu.VMEM((PH, C), BF16),
            pltpu.VMEM((C, HEADS), BF16),
            pltpu.VMEM((D, D), BF16),
            pltpu.VMEM((D, D), BF16),
            pltpu.VMEM((D, D), BF16),
            pltpu.VMEM((D, D), BF16),
            pltpu.VMEM((D, C), BF16),
            pltpu.VMEM((C_DEV, 32, 256), BF16),
            pltpu.VMEM((D, 256), BF16),
            pltpu.VMEM((NI, D), BF16),
            pltpu.VMEM((NJ, 2 * D), F32),
            pltpu.VMEM((2, 16 * NJ, 512), BF16),
            pltpu.VMEM((2, 16 * NJ, 512), BF16),
            pltpu.VMEM((2, NI, 16 * NJ), BF16),
            pltpu.VMEM((OWNERS, OWN, WL), BF16),
            pltpu.VMEM((C_DEV, OWN, WL), BF16),
            pltpu.VMEM((C_DEV, 2, OWN, 128), BF16),
            pltpu.VMEM((OWNERS, 2, OWN, 128), BF16),
            pltpu.VMEM((OWN, 128), BF16),
            pltpu.VMEM((6, OWN, 128), BF16),
            dma((9,)),
            dma((NI // RC,)),
            dma, dma, dma, dma, dma, dma, dma, dma, dma,
        ],
        compiler_params=pltpu.CompilerParams(
            collective_id=0, has_side_effects=True, vmem_limit_bytes=60 * 1024 * 1024
        ),
        name="trunk_main",
    )(pair, seq, w_hidden, w_back, w_bias, w_query, w_key, w_value, w_out, w_project)
    step = 16
    pair_out = pl.pallas_call(
        pair_kernel,
        out_shape=jax.ShapeDtypeStruct((NI, NJ, C), BF16),
        grid=(NI // step,),
        in_specs=[
            pl.BlockSpec((step, NJ, C), lambda i: (i, 0, 0)),
            pl.BlockSpec((step, 128), lambda i: (i, 0)),
            pl.BlockSpec((NJ, 128), lambda i: (0, 0)),
            pl.BlockSpec((C, C), lambda i: (0, 0)),
        ],
        out_specs=pl.BlockSpec((step, NJ, C), lambda i: (i, 0, 0)),
        compiler_params=pltpu.CompilerParams(dimension_semantics=("arbitrary",)),
        name="pair_update",
    )(mid, left, right, w_pair)
    return pair_out, seq_new


def solution(mesh):
    return jax.shard_map(
        local,
        mesh=mesh,
        in_specs=(P("row", "col", None), P(None, "col")) + (P(),) * 9,
        out_specs=(P("row", "col", None), P("row", "col")),
        check_vma=False,
    )
```

time: 182 us -> 67 us (0.37)
  the two profiles are of different devices: /device:TPU:1 before, /device:TPU:17 now
where the time goes in v1:
time: 67 us; the launch traced here: 66.7 us
  Pallas kernels  62.1 us (93%)
  local copies, waits for them, and re-layouts  3.92 us (6%)
    pallas_call x1, Pallas kernels, local(): pl.pallas_call(main_kernel, out_shape=(jax.ShapeDtypeStruct((NI, NJ, C),...  53.5 us
    pallas_call x1, Pallas kernels, local(): pl.pallas_call(pair_kernel, out_shape=jax.ShapeDtypeStruct((NI, NJ, C), B...  8.61 us
    unnamed x5, local copies, waits for them, and re-layouts  3.92 us

profile of v1, /device:TPU:17, one launch (start us, length us, event | category | flops | bytes accessed | tf_op | source)
XLA Modules:
  0.0 66.7 jit_solution(17993862194937557794)
XLA Ops:
  0.6 1.4 %copy.14.wbias_h = bf16[128,32]{1,0:T(8,128)(2,1)} copy(bf16[128,32]{0,1:T(8,128)(2,1)} %param.15) | data formatting | bytes 16384 | tf_op args[4]
  2.0 1.8 %copy.13.seq_h = bf16[1536,32]{1,0:T(8,128)(2,1)} copy(bf16[1536,32]{0,1:T(8,128)(2,1)} %param.12) | data formatting | bytes 196608 | tf_op args[1]
  3.9 53.5 %trunk_main.1 = (bf16[192,48,128]{2,1,0:T(8,128)(2,1)}, f32[192,128]{1,0:T(8,128)}, f32[48,128]{1,0:T(8,128)}, bf16[192,32]{1,0:T(8,128)(2,1)}) custom-call(bf16[192,48,128]{2,1,0:T(8,128)(2,1)} %pair_h.1, bf16[1536,32]{1,0:T(8,128)(2,1)} %copy.13.seq_h, bf16[128,512]{1,0:T(8,128)(2,1)} %whid_h.1, bf16[512,128]{1,0:T(8,128)(2,1)} %wback_h.1, ...), custom_call_target="tpu_custom_call" | custom-call | tf_op jit(solution)/shard_map/trunk_main/pallas_call | solution.py:366
  57.4 0.0 copy-start
  57.4 8.6 %pair_update.1 = bf16[192,48,128]{2,1,0:T(8,128)(2,1)} custom-call(bf16[192,48,128]{2,1,0:T(8,128)(2,1)} %get-tuple-element.6.mid_ref, f32[192,128]{1,0:T(8,128)} %get-tuple-element.7.left_ref, f32[48,128]{1,0:T(8,128)} %get-tuple-element.8.right_ref, bf16[128,128]{1,0:T(8,128)(2,1)} %wpair_ref.1), custom_call_target="tpu_custom_call" | custom-call | tf_op jit(solution)/shard_map/pair_update/pallas_call | solution.py:414
  66.0 0.0 copy-done
  66.0 0.7 %copy.15 = bf16[192,32]{0,1:T(8,128)(2,1)} copy(bf16[192,32]{1,0:T(8,128)(2,1)S(1)} %copy-done) | data formatting | bytes 24576
Async XLA Ops:
  57.4 8.6 %copy-start = (bf16[192,32]{1,0:T(8,128)(2,1)S(1)}, bf16[192,32]{1,0:T(8,128)(2,1)}, u32[]{:S(2)}) copy-start(bf16[192,32]{1,0:T(8,128)(2,1)} %get-tuple-element.11) | copy-start | bytes 36868

commit v2 on v1

v2 whole, which is shorter than its diff:
```python
import functools

import jax
import jax.numpy as jnp
from jax import lax
from jax.experimental import pallas as pl
from jax.experimental.pallas import tpu as pltpu
from jax.sharding import PartitionSpec as P

HEADS = 32
EPS = 1e-05
F32 = jnp.float32
BF16 = jnp.bfloat16

R_DEV, C_DEV = 8, 32
NI, NJ, C, D, PH = 192, 48, 128, 1024, 512
OWNERS, OWN = 24, 8
WL = D + 128
RC = 16
STEPS = NI // RC
BLK = 48
SPB = BLK // RC
KSTEPS = 12
SCALE = 32 ** (-0.5)
MESH = pl.DeviceIdType.MESH


def nt(a, b):
    return lax.dot_general(a, b, (((1,), (1,)), ((), ())), preferred_element_type=F32)


def tn(a, b):
    return lax.dot_general(a, b, (((0,), (0,)), ((), ())), preferred_element_type=F32)


def nn(a, b):
    return jnp.dot(a, b, preferred_element_type=F32)


def layer_norm(x, axis=-1):
    mean = jnp.mean(x, axis=axis, keepdims=True)
    cen = x - mean
    var = jnp.mean(cen * cen, axis=axis, keepdims=True)
    return cen * lax.rsqrt(var + EPS)


def iota(shape, dim):
    return lax.broadcasted_iota(jnp.int32, shape, dim)


def owner_of(col):
    y, x, z = col // 8, (col // 2) % 4, col % 2
    xr = jnp.where(x > y, x - 1, x)
    return (y * 3 + xr) * 2 + z, x != y, y


def col_of(y, t):
    xr, z = t // 2, t % 2
    x = jnp.where(xr >= y, xr + 1, xr)
    return (y * 4 + x) * 2 + z


def main_kernel(
    pair_h, seq_h, whid_h, wback_h, wbias_h, wq_h, wk_h, wv_h, wout_h, wproj_h,
    mid_h, left_o, right_o, seq_o,
    pair_v, mid_v, nb0, nb1, mb0, mb1, mn0, mn1, bias_v, bmat_v,
    seq_v, whid_v, wback_v, wbias_v, wq_v, wk_v, wv_v, wout_v, wproj_v,
    msgs, sqk, sqn, q_v, kv_v, kbd, vbd, w_v, expand_v, wmsg, wrecv, emsg, erecv, rmsg, rrecv,
    in_sem, pin_sem, mid_sem, s_send, s_recv, w_send, w_recv, e_send, e_recv, r_send, r_recv,
):
    me_r, me_c = lax.axis_index("row"), lax.axis_index("col")
    own_o, is_owner, me_y = owner_of(me_c)
    own_o = jnp.where(is_owner, own_o, 0)
    dest_c = 4 * me_r + me_y
    self_right = jnp.logical_and(is_owner, dest_c == me_c)

    barrier = pltpu.get_barrier_semaphore()

    def greet(s, _):
        pl.semaphore_signal(barrier, 1, device_id=(me_r, (me_c + s) % C_DEV), device_id_type=MESH)
        return 0

    lax.fori_loop(1, C_DEV, greet, 0)
    src_r, src_y = me_c // 4, me_c % 4

    def greet_right(t, _):
        src = col_of(src_y, t)

        @pl.when(jnp.logical_not(jnp.logical_and(src_r == me_r, src == me_c)))
        def _():
            pl.semaphore_signal(barrier, 1, device_id=(src_r, src), device_id_type=MESH)

        return 0

    lax.fori_loop(0, 6, greet_right, 0)

    def load(src, dst, k):
        cp = pltpu.make_async_copy(src, dst, in_sem.at[k])
        cp.start()
        return cp

    def block_y(cc):
        return (me_y + 1 + cc) % 4

    def true_rows(k):
        return pl.ds(pl.multiple_of(block_y(k // SPB) * BLK + (k % SPB) * RC, RC), RC)

    c_seq = load(seq_h, seq_v, 0)
    c_hid = load(whid_h, whid_v, 1)
    c_back = load(wback_h, wback_v, 2)
    c_bias = load(wbias_h, wbias_v, 3)

    def pair_copy(k):
        rows = pl.ds(pl.multiple_of(k * RC, RC), RC)
        return pltpu.make_async_copy(pair_h.at[true_rows(k)], pair_v.at[rows], pin_sem.at[k])

    for k in range(STEPS):
        pair_copy(k).start()
    c_q = load(wq_h, wq_v, 4)
    c_k = load(wk_h, wk_v, 5)
    c_v = load(wv_h, wv_v, 6)
    c_out = load(wout_h, wout_v, 7)
    c_proj = load(wproj_h, wproj_v, 8)

    c_seq.wait()
    lane32 = iota((32, 128), 1)
    base = pl.multiple_of((me_r * 3 // 2) * 128, 128)
    own = seq_v[:, pl.ds(base, 256)].astype(F32)
    own = jnp.where(me_r % 2 == 1, pltpu.roll(own, 192, 1), own)
    own0, own1 = own[:, 0:128].astype(BF16), own[:, 128:256]
    for c in range(C_DEV):
        t, o = (c * NJ) // 128, (c * NJ) % 128
        keys = seq_v[:, t * 128 : t * 128 + 128].astype(F32)
        if o + NJ > 128:
            keys = jnp.where(lane32 >= o, keys, seq_v[:, t * 128 + 128 : t * 128 + 256].astype(F32))
        if o != 64:
            keys = pltpu.roll(keys, (64 - o) % 128, 1)
        msgs[c, :, 0:128] = own0
        msgs[c, :, 128:256] = jnp.where(lane32 < 64, own1, jnp.where(lane32 < 112, keys, 0.0)).astype(BF16)

    c_bias.wait()
    spread = jnp.where(
        iota((32, 256), 0) == (iota((32, 256), 1) // 128) * 16 + iota((32, 256), 1) % 16, 1.0, 0.0
    ).astype(BF16)
    wide = tn(wbias_v[...], spread)
    slot = (iota((C, 256), 1) % 128) // 16
    for j8 in range(8):
        bmat_v[j8 * C : (j8 + 1) * C, :] = jnp.where(slot == j8, wide, 0.0).astype(BF16)
    head_lane = iota((128, D), 0) == iota((128, D), 1) // 32
    expand_v[0:128] = jnp.where(head_lane, 1.0, 0.0).astype(BF16)
    expand_v[128:256] = jnp.where(head_lane, 1.0, 0.0).astype(BF16)

    nb, mb, mn = (nb0, nb1), (mb0, mb1), (mn0, mn1)

    def rows_of(k):
        return pl.ds(pl.multiple_of(k * RC, RC), RC)

    def stage_norm(k, s):
        pair_copy(k).wait()
        x = pair_v[rows_of(k)].astype(F32).reshape(RC * NJ, C)
        nb[s][...] = layer_norm(x).astype(BF16)

    def stage_hidden(k, s):
        hid = jnp.maximum(nn(nb[s][...], whid_v[...]), 0.0).astype(BF16)
        x = pair_v[rows_of(k)].astype(F32).reshape(RC * NJ, C)
        mid = (x + nn(hid, wback_v[...])).astype(BF16)
        mid_v[rows_of(k)] = mid.reshape(RC, NJ, C)
        mb[s][...] = mid

    def stage_mid(k, s):
        mn[s][...] = layer_norm(mb[s][...].astype(F32))

    def stage_bias(k, s):
        blocks = []
        for jb in range(6):
            cols = []
            for j8 in range(8):
                j = jb * 8 + j8
                cols.append(
                    jnp.concatenate(
                        [mn[s][pl.ds(h * 8 * NJ + j, 8, stride=NJ), :] for h in range(RC // 8)], axis=0
                    ).astype(BF16)
                )
            blocks.append(jnp.concatenate(cols, axis=1))
        out = nn(jnp.concatenate(blocks, axis=0), bmat_v[...])
        for jb in range(6):
            for g in range(2):
                bias_v[g, jb, rows_of(k), :] = out[jb * RC : (jb + 1) * RC, g * 128 : (g + 1) * 128]

    def mid_out(k):
        return pltpu.make_async_copy(mid_v.at[rows_of(k)], mid_h.at[true_rows(k)], mid_sem)

    def pair_steps(t, _):
        for u in range(2):
            k, s = 2 * t + 1 + u, (1 + u) % 2
            stage_hidden(k, s)
            stage_norm(k + 1, 1 - s)
            stage_mid(k - 1, 1 - s)
            stage_bias(jnp.maximum(k - 2, 0), s)
            mid_out(k - 1).start()
        return 0

    c_hid.wait()
    c_back.wait()
    stage_norm(0, 0)
    stage_hidden(0, 0)
    stage_norm(1, 1)
    mn[1][...] = jnp.zeros_like(mn[1])

    pl.semaphore_wait(
        barrier, C_DEV - 1 + jnp.where(is_owner, R_DEV, 0) - jnp.where(self_right, 1, 0)
    )
    my_slab = pl.ds(pl.multiple_of(me_c * 32, 32), 32)

    def send_seq(s, _):
        dst = (me_c + s) % C_DEV
        pltpu.make_async_remote_copy(
            msgs.at[dst], sqk.at[my_slab], s_send, s_recv, device_id=(me_r, dst), device_id_type=MESH
        ).start()
        return 0

    lax.fori_loop(1, C_DEV, send_seq, 0)
    pltpu.make_async_copy(msgs.at[me_c], sqk.at[my_slab], s_recv).start()

    lax.fori_loop(0, 4, pair_steps, 0)

    pltpu.make_async_copy(sqk, sqk, s_recv).wait()
    CH = 128

    def chunk(k):
        return sqk[pl.ds(pl.multiple_of(k * CH, CH), CH), :].astype(F32).reshape(CH // 8, 8, 256)

    def add_sum(k, acc):
        return acc + jnp.sum(chunk(k), axis=0)

    mean = jnp.sum(lax.fori_loop(0, D // CH, add_sum, jnp.zeros((8, 256), F32)), axis=0, keepdims=True) * (1.0 / D)

    def add_square(k, acc):
        cen = chunk(k) - mean[None]
        return acc + jnp.sum(cen * cen, axis=0)

    var = jnp.sum(lax.fori_loop(0, D // CH, add_square, jnp.zeros((8, 256), F32)), axis=0, keepdims=True) * (1.0 / D)
    inv = lax.rsqrt(var + EPS)

    def norm_chunk(k, _):
        sqn[pl.ds(pl.multiple_of(k * CH, CH), CH), :] = (
            ((chunk(k) - mean[None]) * inv[None]).reshape(CH, 256).astype(BF16)
        )
        return 0

    lax.fori_loop(0, D // CH, norm_chunk, 0)
    ident = jnp.where(iota((256, 256), 0) == iota((256, 256), 1), 1.0, 0.0).astype(BF16)
    normed = nt(ident, sqn[...]).astype(BF16)
    c_q.wait()
    q_v[...] = nn(normed[:NI], wq_v[...]).astype(BF16)
    c_k.wait()
    c_v.wait()
    kv_v[:, 0:D] = nn(normed[NI : NI + NJ], wk_v[...])
    kv_v[:, D : 2 * D] = nn(normed[NI : NI + NJ], wv_v[...])
    head_here = iota((16, 512), 0) == iota((16, 512), 1) // 32

    def spread_keys(j, _):
        dst = pl.ds(pl.multiple_of(j * 16, 16), 16)
        for g in range(2):
            krow = jnp.broadcast_to(kv_v[pl.ds(j, 1), g * 512 : (g + 1) * 512], (16, 512))
            vrow = jnp.broadcast_to(kv_v[pl.ds(j, 1), D + g * 512 : D + (g + 1) * 512], (16, 512))
            kbd[g, dst, :] = jnp.where(head_here, krow, 0.0).astype(BF16)
            vbd[g, dst, :] = jnp.where(head_here, vrow, 0.0).astype(BF16)
        return 0

    lax.fori_loop(0, NJ, spread_keys, 0)

    def attend(first, count):
        n = count * BLK
        lane = iota((n, 128), 1)
        q = [
            q_v[pl.ds(pl.multiple_of(block_y(cc) * BLK, 16), BLK), :] for cc in range(first, first + count)
        ]
        q = q[0] if count == 1 else jnp.concatenate(q, axis=0)
        here = slice(first * BLK, first * BLK + n)
        parts = []
        for g in range(2):
            scores = nt(q[:, g * 512 : (g + 1) * 512], kbd[g])
            tiles = [scores[:, jb * 128 : (jb + 1) * 128] * SCALE + bias_v[g, jb, here, :] for jb in range(6)]
            top = functools.reduce(jnp.maximum, tiles)
            for shift in (16, 32, 64):
                top = jnp.maximum(top, pltpu.roll(top, shift, 1))
            total = None
            for jb in range(6):
                w = jnp.exp(tiles[jb] - top)
                w_v[g, here, jb * 128 : (jb + 1) * 128] = w.astype(BF16)
                total = w if total is None else total + w
            for shift in (16, 32, 64):
                total = total + pltpu.roll(total, shift, 1)
            weighted = nn(w_v[g, here, :], vbd[g])
            wmsg[first * 6 : (first + count) * 6, :, g * 512 : (g + 1) * 512] = weighted.reshape(
                count * 6, OWN, 512
            ).astype(BF16)
            high = top.astype(BF16).astype(F32)
            middle = (top - high).astype(BF16).astype(F32)
            low = (top - high) - middle
            parts.append((high, middle, low, total))
        stats = jnp.zeros((n, 128), F32)
        for p in range(4):
            for g in range(2):
                stats = jnp.where(lane // 16 == p * 2 + g, parts[g][p], stats)
        wmsg[first * 6 : (first + count) * 6, :, D:WL] = stats.reshape(count * 6, OWN, 128).astype(BF16)

        def send_rows(i, _):
            cc, t = first + i // 6, i % 6
            dst = col_of(block_y(cc), t)
            mine = dst == me_c

            @pl.when(jnp.logical_not(mine))
            def _():
                pltpu.make_async_remote_copy(
                    wmsg.at[cc * 6 + t], wrecv.at[me_c], w_send, w_recv,
                    device_id=(me_r, dst), device_id_type=MESH,
                ).start()

            @pl.when(mine)
            def _():
                pltpu.make_async_copy(wmsg.at[cc * 6 + t], wrecv.at[me_c], w_recv).start()

            return 0

        lax.fori_loop(0, count * 6, send_rows, 0)

    attend(0, 2)
    pair_steps(4, 0)
    attend(2, 1)
    stage_hidden(11, 1)
    stage_mid(10, 0)
    stage_bias(9, 1)
    stage_mid(11, 1)
    stage_bias(10, 0)
    stage_bias(11, 1)
    mid_out(10).start()
    mid_out(11).start()
    attend(3, 1)

    @pl.when(is_owner)
    def _():
        pick = jnp.where(iota((8, 256), 1) == own_o * 8 + iota((8, 256), 0), 1.0, 0.0).astype(BF16)
        resid = nt(pick, sqk[...])
        c_out.wait()
        c_proj.wait()
        pltpu.make_async_copy(wrecv, wrecv, w_recv).wait()
        st = wrecv[:, :, D:WL].astype(F32).reshape(C_DEV * OWN, 128)
        m = (st + pltpu.roll(st, 96, 1)) + pltpu.roll(st, 64, 1)
        den = pltpu.roll(st, 32, 1)
        m3 = m.reshape(C_DEV, OWN, 128)
        top = jnp.max(m3, axis=0)
        fac = jnp.where(iota((C_DEV, OWN, 128), 2) < 32, jnp.exp(jnp.minimum(m3 - top[None], 0.0)), 0.0)
        whole = jnp.sum(fac * den.reshape(C_DEV, OWN, 128), axis=0)
        whole = jnp.where(iota((OWN, 128), 1) < 32, whole, 1.0)
        fac = (fac / whole[None]).reshape(C_DEV * OWN, 128)
        high = fac.astype(BF16)
        low = (fac - high.astype(F32)).astype(BF16)
        wide = nn(jnp.concatenate([high, low], axis=1), expand_v[...]).reshape(C_DEV, OWN, D)
        attended = jnp.sum(wide * wrecv[:, :, 0:D].astype(F32), axis=0).astype(BF16)
        seq_new = (resid + nn(attended, wout_v[...])).astype(BF16).astype(F32)
        proj = nn(layer_norm(seq_new).astype(BF16), wproj_v[...]).astype(BF16).astype(F32)
        turned = pltpu.roll(proj, 64, 1)
        lane8 = iota((OWN, 128), 1)
        left = jnp.where(lane8 < 64, proj, turned).astype(BF16)
        right = jnp.where(lane8 < 64, turned, proj).astype(BF16)
        rmsg[...] = right
        for c in range(C_DEV):
            tile = seq_new[:, (c // 4) * 128 : (c // 4) * 128 + 128]
            if c % 4:
                tile = pltpu.roll(tile, 128 - 32 * (c % 4), 1)
            emsg[c, 0] = left
            emsg[c, 1] = tile.astype(BF16)

        def send_right(r, _):
            here = jnp.logical_and(r == me_r, dest_c == me_c)

            @pl.when(jnp.logical_not(here))
            def _():
                pltpu.make_async_remote_copy(
                    rmsg, rrecv.at[own_o % 6], r_send, r_recv, device_id=(r, dest_c), device_id_type=MESH
                ).start()

            @pl.when(here)
            def _():
                pltpu.make_async_copy(rmsg, rrecv.at[own_o % 6], r_recv).start()

            return 0

        lax.fori_loop(0, R_DEV, send_right, 0)

        def send_left(s, _):
            dst = (me_c + s) % C_DEV
            pltpu.make_async_remote_copy(
                emsg.at[dst], erecv.at[own_o], e_send, e_recv, device_id=(me_r, dst), device_id_type=MESH
            ).start()
            return 0

        lax.fori_loop(1, C_DEV, send_left, 0)
        pltpu.make_async_copy(emsg.at[me_c], erecv.at[own_o], e_recv).start()

    @pl.when(jnp.logical_not(is_owner))
    def _():
        c_out.wait()
        c_proj.wait()

    pltpu.make_async_copy(mid_v, mid_h, mid_sem).wait()
    pltpu.make_async_copy(msgs.at[0 : C_DEV - 1], msgs.at[0 : C_DEV - 1], s_send).wait()

    def sent_rows(i, _):
        @pl.when(col_of(block_y(i // 6), i % 6) != me_c)
        def _():
            pltpu.make_async_copy(wmsg.at[i], wmsg.at[i], w_send).wait()

        return 0

    lax.fori_loop(0, OWNERS, sent_rows, 0)

    pltpu.make_async_copy(rrecv, rrecv, r_recv).wait()
    right_o[...] = rrecv[...].astype(F32).reshape(NJ, 128)
    pltpu.make_async_copy(erecv, erecv, e_recv).wait()
    left_o[...] = erecv[:, 0].astype(F32).reshape(NI, 128)
    eye = jnp.where(iota((32, 128), 0) == iota((32, 128), 1), 1.0, 0.0).astype(BF16)
    seq_o[...] = nt(eye, erecv[:, 1].astype(F32).reshape(NI, 128).astype(BF16)).astype(BF16)

    @pl.when(is_owner)
    def _():
        pltpu.make_async_copy(emsg.at[0 : C_DEV - 1], emsg.at[0 : C_DEV - 1], e_send).wait()

        def sent_right(r, _):
            @pl.when(jnp.logical_not(jnp.logical_and(r == me_r, dest_c == me_c)))
            def _():
                pltpu.make_async_copy(rmsg, rmsg, r_send).wait()

            return 0

        lax.fori_loop(0, R_DEV, sent_right, 0)


def pair_kernel(mid_h, left_ref, right_ref, wpair_ref, out_h, mid_v, out_v, in_sem, out_sem):
    n = NI // KSTEPS

    def rows(k):
        return pl.ds(pl.multiple_of(k * n, n), n)

    def fetch(k):
        return pltpu.make_async_copy(mid_h.at[rows(k)], mid_v.at[rows(k)], in_sem.at[k])

    def put(k):
        return pltpu.make_async_copy(out_v.at[rows(k)], out_h.at[rows(k)], out_sem)

    for k in range(KSTEPS):
        fetch(k).start()
    lane = iota((NJ, C), 1)
    right = right_ref[...]
    scale = jnp.where(lane < 64, right, 1.0)
    shift = jnp.where(lane < 64, 0.0, -right)

    def step(k, _):
        fetch(k).wait()
        left = left_ref[rows(k), :].reshape(n, 1, C)
        feature = (left * scale[None] + shift[None]).astype(BF16).reshape(n * NJ, C)
        update = nn(feature, wpair_ref[...])
        mid = mid_v[rows(k)].astype(F32).reshape(n * NJ, C)
        out_v[rows(k)] = (mid + update).astype(BF16).reshape(n, NJ, C)
        put(k).start()
        return 0

    lax.fori_loop(0, KSTEPS, step, 0)
    pltpu.make_async_copy(out_v, out_h, out_sem).wait()


def local(pair, seq, w_hidden, w_back, w_bias, w_query, w_key, w_value, w_out, w_project, w_pair):
    hbm = pl.BlockSpec(memory_space=pl.ANY)
    vmem = pl.BlockSpec(memory_space=pltpu.VMEM)
    dma = pltpu.SemaphoreType.DMA
    mid, left, right, seq_new = pl.pallas_call(
        main_kernel,
        out_shape=(
            jax.ShapeDtypeStruct((NI, NJ, C), BF16),
            jax.ShapeDtypeStruct((NI, 128), F32),
            jax.ShapeDtypeStruct((NJ, 128), F32),
            jax.ShapeDtypeStruct((32, NI), BF16),
        ),
        in_specs=[hbm] * 10,
        out_specs=(hbm, vmem, vmem, vmem),
        scratch_shapes=[
            pltpu.VMEM((NI, NJ, C), BF16),
            pltpu.VMEM((NI, NJ, C), BF16),
            pltpu.VMEM((RC * NJ, C), BF16),
            pltpu.VMEM((RC * NJ, C), BF16),
            pltpu.VMEM((RC * NJ, C), BF16),
            pltpu.VMEM((RC * NJ, C), BF16),
            pltpu.VMEM((RC * NJ, C), F32),
            pltpu.VMEM((RC * NJ, C), F32),
            pltpu.VMEM((2, 6, NI, 128), F32),
            pltpu.VMEM((8 * C, 256), BF16),
            pltpu.VMEM((32, R_DEV * NI), BF16),
            pltpu.VMEM((C, PH), BF16),
            pltpu.VMEM((PH, C), BF16),
            pltpu.VMEM((HEADS, C), BF16),
            pltpu.VMEM((D, D), BF16),
            pltpu.VMEM((D, D), BF16),
            pltpu.VMEM((D, D), BF16),
            pltpu.VMEM((D, D), BF16),
            pltpu.VMEM((D, C), BF16),
            pltpu.VMEM((C_DEV, 32, 256), BF16),
            pltpu.VMEM((D, 256), BF16),
            pltpu.VMEM((D, 256), BF16),
            pltpu.VMEM((NI, D), BF16),
            pltpu.VMEM((NJ, 2 * D), F32),
            pltpu.VMEM((2, 16 * NJ, 512), BF16),
            pltpu.VMEM((2, 16 * NJ, 512), BF16),
            pltpu.VMEM((2, NI, 16 * NJ), BF16),
            pltpu.VMEM((256, D), BF16),
            pltpu.VMEM((OWNERS, OWN, WL), BF16),
            pltpu.VMEM((C_DEV, OWN, WL), BF16),
            pltpu.VMEM((C_DEV, 2, OWN, 128), BF16),
            pltpu.VMEM((OWNERS, 2, OWN, 128), BF16),
            pltpu.VMEM((OWN, 128), BF16),
            pltpu.VMEM((6, OWN, 128), BF16),
            dma((9,)),
            dma((STEPS,)),
            dma, dma, dma, dma, dma, dma, dma, dma, dma,
        ],
        compiler_params=pltpu.CompilerParams(
            collective_id=0, has_side_effects=True, vmem_limit_bytes=60 * 1024 * 1024
        ),
        name="trunk_main",
    )(pair, seq.T, w_hidden, w_back, w_bias.T, w_query, w_key, w_value, w_out, w_project)
    pair_out = pl.pallas_call(
        pair_kernel,
        out_shape=jax.ShapeDtypeStruct((NI, NJ, C), BF16),
        in_specs=[hbm, vmem, vmem, vmem],
        out_specs=hbm,
        scratch_shapes=[
            pltpu.VMEM((NI, NJ, C), BF16),
            pltpu.VMEM((NI, NJ, C), BF16),
            dma((KSTEPS,)),
            dma,
        ],
        compiler_params=pltpu.CompilerParams(vmem_limit_bytes=16 * 1024 * 1024),
        name="pair_update",
    )(mid, left, right, w_pair)
    return pair_out, seq_new.T


def solution(mesh):
    return jax.shard_map(
        local,
        mesh=mesh,
        in_specs=(P("row", "col", None), P(None, "col")) + (P(),) * 9,
        out_specs=(P("row", "col", None), P("row", "col")),
        check_vma=False,
    )
```

time: 67 us -> 53.7 us (0.80)
  the two profiles are of different devices: /device:TPU:17 before, /device:TPU:1 now
where the time goes in v2:
time: 53.7 us; the launch traced here: 53.1 us
  Pallas kernels  48.5 us (90%)
  local copies, waits for them, and re-layouts  3.9 us (7%)
  between operations  0.68 us (1%)
    pallas_call x1, Pallas kernels, local(): pl.pallas_call(main_kernel, out_shape=(jax.ShapeDtypeStruct((NI, NJ, C),...  42.3 us
    pallas_call x1, Pallas kernels, local(): pl.pallas_call(pair_kernel, out_shape=jax.ShapeDtypeStruct((NI, NJ, C), B...  6.22 us
    unnamed x11, local copies, waits for them, and re-layouts  3.9 us

profile of v2, /device:TPU:1, one launch (start us, length us, event | category | flops | bytes accessed | tf_op | source)
XLA Modules:
  0.0 53.1 jit_solution(18330789567007958821)
XLA Ops:
  0.6 0.0 copy-start.2
  0.6 42.3 %trunk_main.1 = (bf16[192,48,128]{2,1,0:T(8,128)(2,1)}, f32[192,128]{1,0:T(8,128)}, f32[48,128]{1,0:T(8,128)}, bf16[32,192]{1,0:T(8,128)(2,1)}) custom-call(bf16[192,48,128]{2,1,0:T(8,128)(2,1)} %pair_h.1, bf16[32,1536]{1,0:T(8,128)(2,1)} %bitcast.3, bf16[128,512]{1,0:T(8,128)(2,1)} %whid_h.1, bf16[512,128]{1,0:T(8,128)(2,1)} %wback_h.1, ...), custom_call_target="tpu_custom_call" | custom-call | tf_op jit(solution)/shard_map/trunk_main/pallas_call | solution.py:478
  42.9 0.0 copy-done.2
  42.9 0.0 copy-start
  42.9 1.7 %copy-done = bf16[192,48,128]{2,1,0:T(8,128)(2,1)S(1)} copy-done((bf16[192,48,128]{2,1,0:T(8,128)(2,1)S(1)}, bf16[192,48,128]{2,1,0:T(8,128)(2,1)}, u32[]{:S(2)}) %copy-start) | copy-done | bytes 2359320
  44.6 0.0 copy-start.1
  44.6 0.9 %copy-done.1 = f32[192,128]{1,0:T(8,128)S(1)} copy-done((f32[192,128]{1,0:T(8,128)S(1)}, f32[192,128]{1,0:T(8,128)}, u32[]{:S(2)}) %copy-start.1) | copy-done | bytes 98328
  45.5 0.0 copy-start.3
  45.5 0.7 %copy-done.3 = f32[48,128]{1,0:T(8,128)S(1)} copy-done((f32[48,128]{1,0:T(8,128)S(1)}, f32[48,128]{1,0:T(8,128)}, u32[]{:S(2)}) %copy-start.3) | copy-done | bytes 24600
  46.2 0.0 copy-start.4
  46.2 6.2 %pair_update.1 = bf16[192,48,128]{2,1,0:T(8,128)(2,1)} custom-call(bf16[192,48,128]{2,1,0:T(8,128)(2,1)S(1)} %copy-done, f32[192,128]{1,0:T(8,128)S(1)} %copy-done.1, f32[48,128]{1,0:T(8,128)S(1)} %copy-done.3, bf16[128,128]{1,0:T(8,128)(2,1)S(1)} %copy-done.2), custom_call_target="tpu_custom_call" | custom-call | tf_op jit(solution)/shard_map/pair_update/pallas_call | solution.py:532
  52.4 0.0 copy-done.4
  52.5 0.6 %copy.14 = bf16[192,32]{0,1:T(8,128)(2,1)} copy(bf16[192,32]{0,1:T(8,128)(2,1)S(1)} %bitcast.4) | data formatting | bytes 24576
Async XLA Ops:
  0.6 42.3 %copy-start.2 = (bf16[128,128]{1,0:T(8,128)(2,1)S(1)}, bf16[128,128]{1,0:T(8,128)(2,1)}, u32[]{:S(2)}) copy-start(bf16[128,128]{1,0:T(8,128)(2,1)} %wpair_ref.1) | copy-start | bytes 98308
  42.9 1.7 %copy-start = (bf16[192,48,128]{2,1,0:T(8,128)(2,1)S(1)}, bf16[192,48,128]{2,1,0:T(8,128)(2,1)}, u32[]{:S(2)}) copy-start(bf16[192,48,128]{2,1,0:T(8,128)(2,1)} %get-tuple-element.6.mid_h) | copy-start | bytes 7077892
  44.6 0.9 %copy-start.1 = (f32[192,128]{1,0:T(8,128)S(1)}, f32[192,128]{1,0:T(8,128)}, u32[]{:S(2)}) copy-start(f32[192,128]{1,0:T(8,128)} %get-tuple-element.7.left_ref) | copy-start | bytes 294916
  45.5 0.7 %copy-start.3 = (f32[48,128]{1,0:T(8,128)S(1)}, f32[48,128]{1,0:T(8,128)}, u32[]{:S(2)}) copy-start(f32[48,128]{1,0:T(8,128)} %get-tuple-element.8.right_ref) | copy-start | bytes 73732
  46.2 6.2 %copy-start.4 = (bf16[32,192]{1,0:T(8,128)(2,1)S(1)}, bf16[32,192]{1,0:T(8,128)(2,1)}, u32[]{:S(2)}) copy-start(bf16[32,192]{1,0:T(8,128)(2,1)} %get-tuple-element.9) | copy-start | bytes 36868

commit v3 on v2

--- a/solution.py
+++ b/solution.py
@@ -20,7 +20,7 @@
 STEPS = NI // RC
 BLK = 48
 SPB = BLK // RC
-KSTEPS = 12
+KSTEPS = 4
 SCALE = 32 ** (-0.5)
 MESH = pl.DeviceIdType.MESH
 
@@ -49,13 +49,13 @@
 
 
 def owner_of(col):
-    y, x, z = col // 8, (col // 2) % 4, col % 2
+    y, x, z = lax.div(col, 8), lax.rem(lax.div(col, 2), 4), lax.rem(col, 2)
     xr = jnp.where(x > y, x - 1, x)
     return (y * 3 + xr) * 2 + z, x != y, y
 
 
 def col_of(y, t):
-    xr, z = t // 2, t % 2
+    xr, z = (t // 2, t % 2) if isinstance(t, int) else (lax.div(t, 2), lax.rem(t, 2))
     x = jnp.where(xr >= y, xr + 1, xr)
     return (y * 4 + x) * 2 + z
 
@@ -63,9 +63,9 @@
 def main_kernel(
     pair_h, seq_h, whid_h, wback_h, wbias_h, wq_h, wk_h, wv_h, wout_h, wproj_h,
     mid_h, left_o, right_o, seq_o,
-    pair_v, mid_v, nb0, nb1, mb0, mb1, mn0, mn1, bias_v, bmat_v,
+    pair_v, mid_v, nb0, nb1, nb2, mb0, mb1, mb2, mn_v, bias_v, bmat_v,
     seq_v, whid_v, wback_v, wbias_v, wq_v, wk_v, wv_v, wout_v, wproj_v,
-    msgs, sqk, sqn, q_v, kv_v, kbd, vbd, w_v, expand_v, wmsg, wrecv, emsg, erecv, rmsg, rrecv,
+    msgs, sqk, raw_v, sqn, q_v, kv_v, kbd, vbd, w_v, expand_v, wmsg, wrecv, emsg, erecv, rmsg, rrecv,
     in_sem, pin_sem, mid_sem, s_send, s_recv, w_send, w_recv, e_send, e_recv, r_send, r_recv,
 ):
     me_r, me_c = lax.axis_index("row"), lax.axis_index("col")
@@ -74,36 +74,18 @@
     dest_c = 4 * me_r + me_y
     self_right = jnp.logical_and(is_owner, dest_c == me_c)
 
-    barrier = pltpu.get_barrier_semaphore()
-
-    def greet(s, _):
-        pl.semaphore_signal(barrier, 1, device_id=(me_r, (me_c + s) % C_DEV), device_id_type=MESH)
-        return 0
-
-    lax.fori_loop(1, C_DEV, greet, 0)
-    src_r, src_y = me_c // 4, me_c % 4
-
-    def greet_right(t, _):
-        src = col_of(src_y, t)
-
-        @pl.when(jnp.logical_not(jnp.logical_and(src_r == me_r, src == me_c)))
-        def _():
-            pl.semaphore_signal(barrier, 1, device_id=(src_r, src), device_id_type=MESH)
-
-        return 0
-
-    lax.fori_loop(0, 6, greet_right, 0)
-
     def load(src, dst, k):
         cp = pltpu.make_async_copy(src, dst, in_sem.at[k])
         cp.start()
         return cp
 
     def block_y(cc):
-        return (me_y + 1 + cc) % 4
+        return lax.rem(me_y + 1 + cc, 4)
 
     def true_rows(k):
-        return pl.ds(pl.multiple_of(block_y(k // SPB) * BLK + (k % SPB) * RC, RC), RC)
+        if isinstance(k, int):
+            return pl.ds(pl.multiple_of(block_y(k // SPB) * BLK + (k % SPB) * RC, RC), RC)
+        return pl.ds(pl.multiple_of(block_y(lax.div(k, SPB)) * BLK + lax.rem(k, SPB) * RC, RC), RC)
 
     c_seq = load(seq_h, seq_v, 0)
     c_hid = load(whid_h, whid_v, 1)
@@ -121,6 +103,20 @@
     c_v = load(wv_h, wv_v, 6)
     c_out = load(wout_h, wout_v, 7)
     c_proj = load(wproj_h, wproj_v, 8)
+
+    barrier = pltpu.get_barrier_semaphore()
+    src_r, src_y = lax.div(me_c, 4), lax.rem(me_c, 4)
+    for t in range(6):
+        src = col_of(src_y, t)
+
+        @pl.when(jnp.logical_not(jnp.logical_and(src_r == me_r, src == me_c)))
+        def _():
+            pl.semaphore_signal(barrier, 1, device_id=(src_r, src), device_id_type=MESH)
+
+    for s in range(1, C_DEV):
+        pl.semaphore_signal(
+            barrier, 1, device_id=(me_r, lax.rem(me_c + s, C_DEV)), device_id_type=MESH
+        )
 
     c_seq.wait()
     lane32 = iota((32, 128), 1)
@@ -150,13 +146,12 @@
     expand_v[0:128] = jnp.where(head_lane, 1.0, 0.0).astype(BF16)
     expand_v[128:256] = jnp.where(head_lane, 1.0, 0.0).astype(BF16)
 
-    nb, mb, mn = (nb0, nb1), (mb0, mb1), (mn0, mn1)
+    nb, mb = (nb0, nb1, nb2), (mb0, mb1, mb2)
 
     def rows_of(k):
         return pl.ds(pl.multiple_of(k * RC, RC), RC)
 
     def stage_norm(k, s):
-        pair_copy(k).wait()
         x = pair_v[rows_of(k)].astype(F32).reshape(RC * NJ, C)
         nb[s][...] = layer_norm(x).astype(BF16)
 
@@ -167,10 +162,10 @@
         mid_v[rows_of(k)] = mid.reshape(RC, NJ, C)
         mb[s][...] = mid
 
-    def stage_mid(k, s):
-        mn[s][...] = layer_norm(mb[s][...].astype(F32))
-
-    def stage_bias(k, s):
+    def stage_mid(s):
+        mn_v[s * RC * NJ : (s + 1) * RC * NJ] = layer_norm(mb[s][...].astype(F32))
+
+    def stage_bias(b):
         blocks = []
         for jb in range(6):
             cols = []
@@ -178,97 +173,84 @@
                 j = jb * 8 + j8
                 cols.append(
                     jnp.concatenate(
-                        [mn[s][pl.ds(h * 8 * NJ + j, 8, stride=NJ), :] for h in range(RC // 8)], axis=0
+                        [mn_v[pl.ds(h * 8 * NJ + j, 8, stride=NJ), :] for h in range(BLK // 8)], axis=0
                     ).astype(BF16)
                 )
             blocks.append(jnp.concatenate(cols, axis=1))
         out = nn(jnp.concatenate(blocks, axis=0), bmat_v[...])
         for jb in range(6):
             for g in range(2):
-                bias_v[g, jb, rows_of(k), :] = out[jb * RC : (jb + 1) * RC, g * 128 : (g + 1) * 128]
+                bias_v[g, jb, pl.ds(pl.multiple_of(b * BLK, BLK), BLK), :] = out[
+                    jb * BLK : (jb + 1) * BLK, g * 128 : (g + 1) * 128
+                ]
 
     def mid_out(k):
         return pltpu.make_async_copy(mid_v.at[rows_of(k)], mid_h.at[true_rows(k)], mid_sem)
 
-    def pair_steps(t, _):
-        for u in range(2):
-            k, s = 2 * t + 1 + u, (1 + u) % 2
+    def pair_block(t, _):
+        for u in range(3):
+            pair_copy(3 * t + 2 + u).wait()
+        for u in range(3):
+            k, s = 3 * t + 1 + u, (1 + u) % 3
             stage_hidden(k, s)
-            stage_norm(k + 1, 1 - s)
-            stage_mid(k - 1, 1 - s)
-            stage_bias(jnp.maximum(k - 2, 0), s)
-            mid_out(k - 1).start()
+            stage_norm(k + 1, (s + 1) % 3)
+            stage_mid(u)
+        stage_bias(t)
+        for u in range(3):
+            mid_out(3 * t + u).start()
         return 0
 
     c_hid.wait()
     c_back.wait()
-    stage_norm(0, 0)
-    stage_hidden(0, 0)
-    stage_norm(1, 1)
-    mn[1][...] = jnp.zeros_like(mn[1])
-
+    pair_copy(0).wait()
+    pair_copy(1).wait()
     pl.semaphore_wait(
         barrier, C_DEV - 1 + jnp.where(is_owner, R_DEV, 0) - jnp.where(self_right, 1, 0)
     )
     my_slab = pl.ds(pl.multiple_of(me_c * 32, 32), 32)
-
-    def send_seq(s, _):
-        dst = (me_c + s) % C_DEV
+    for s in range(1, C_DEV):
+        dst = lax.rem(me_c + s, C_DEV)
         pltpu.make_async_remote_copy(
             msgs.at[dst], sqk.at[my_slab], s_send, s_recv, device_id=(me_r, dst), device_id_type=MESH
         ).start()
+    pltpu.make_async_copy(msgs.at[me_c], sqk.at[my_slab], s_recv).start()
+    stage_norm(0, 0)
+    stage_hidden(0, 0)
+    stage_norm(1, 1)
+
+    lax.fori_loop(0, 3, pair_block, 0)
+
+    pltpu.make_async_copy(sqk, sqk, s_recv).wait()
+    ident = jnp.where(iota((256, 256), 0) == iota((256, 256), 1), 1.0, 0.0).astype(BF16)
+    raw_v[...] = nt(ident, sqk[...])
+
+    def norm_rows(k, _):
+        for u in range(4):
+            rows = pl.ds(pl.multiple_of(k * 64 + u * 16, 16), 16)
+            sqn[rows, :] = layer_norm(raw_v[rows, :]).astype(BF16)
         return 0
 
-    lax.fori_loop(1, C_DEV, send_seq, 0)
-    pltpu.make_async_copy(msgs.at[me_c], sqk.at[my_slab], s_recv).start()
-
-    lax.fori_loop(0, 4, pair_steps, 0)
-
-    pltpu.make_async_copy(sqk, sqk, s_recv).wait()
-    CH = 128
-
-    def chunk(k):
-        return sqk[pl.ds(pl.multiple_of(k * CH, CH), CH), :].astype(F32).reshape(CH // 8, 8, 256)
-
-    def add_sum(k, acc):
-        return acc + jnp.sum(chunk(k), axis=0)
-
-    mean = jnp.sum(lax.fori_loop(0, D // CH, add_sum, jnp.zeros((8, 256), F32)), axis=0, keepdims=True) * (1.0 / D)
-
-    def add_square(k, acc):
-        cen = chunk(k) - mean[None]
-        return acc + jnp.sum(cen * cen, axis=0)
-
-    var = jnp.sum(lax.fori_loop(0, D // CH, add_square, jnp.zeros((8, 256), F32)), axis=0, keepdims=True) * (1.0 / D)
-    inv = lax.rsqrt(var + EPS)
-
-    def norm_chunk(k, _):
-        sqn[pl.ds(pl.multiple_of(k * CH, CH), CH), :] = (
-            ((chunk(k) - mean[None]) * inv[None]).reshape(CH, 256).astype(BF16)
-        )
-        return 0
-
-    lax.fori_loop(0, D // CH, norm_chunk, 0)
-    ident = jnp.where(iota((256, 256), 0) == iota((256, 256), 1), 1.0, 0.0).astype(BF16)
-    normed = nt(ident, sqn[...]).astype(BF16)
+    lax.fori_loop(0, 4, norm_rows, 0)
     c_q.wait()
-    q_v[...] = nn(normed[:NI], wq_v[...]).astype(BF16)
+    q_v[...] = nn(sqn[:NI], wq_v[...]).astype(BF16)
     c_k.wait()
     c_v.wait()
-    kv_v[:, 0:D] = nn(normed[NI : NI + NJ], wk_v[...])
-    kv_v[:, D : 2 * D] = nn(normed[NI : NI + NJ], wv_v[...])
+    kv_v[:, 0:D] = nn(sqn[NI : NI + NJ], wk_v[...])
+    kv_v[:, D : 2 * D] = nn(sqn[NI : NI + NJ], wv_v[...])
     head_here = iota((16, 512), 0) == iota((16, 512), 1) // 32
 
-    def spread_keys(j, _):
-        dst = pl.ds(pl.multiple_of(j * 16, 16), 16)
-        for g in range(2):
-            krow = jnp.broadcast_to(kv_v[pl.ds(j, 1), g * 512 : (g + 1) * 512], (16, 512))
-            vrow = jnp.broadcast_to(kv_v[pl.ds(j, 1), D + g * 512 : D + (g + 1) * 512], (16, 512))
-            kbd[g, dst, :] = jnp.where(head_here, krow, 0.0).astype(BF16)
-            vbd[g, dst, :] = jnp.where(head_here, vrow, 0.0).astype(BF16)
+    def spread_keys(j4, _):
+        for u in range(4):
+            j = j4 * 4 + u
+            dst = pl.ds(pl.multiple_of(j * 16, 16), 16)
+            for g in range(2):
+                krow = jnp.broadcast_to(kv_v[pl.ds(j, 1), g * 512 : (g + 1) * 512], (16, 512))
+                vrow = jnp.broadcast_to(kv_v[pl.ds(j, 1), D + g * 512 : D + (g + 1) * 512], (16, 512))
+                kbd[g, dst, :] = jnp.where(head_here, krow, 0.0).astype(BF16)
+                vbd[g, dst, :] = jnp.where(head_here, vrow, 0.0).astype(BF16)
         return 0
 
-    lax.fori_loop(0, NJ, spread_keys, 0)
+    lax.fori_loop(0, NJ // 4, spread_keys, 0)
 
     def attend(first, count):
         n = count * BLK
@@ -306,43 +288,42 @@
                 stats = jnp.where(lane // 16 == p * 2 + g, parts[g][p], stats)
         wmsg[first * 6 : (first + count) * 6, :, D:WL] = stats.reshape(count * 6, OWN, 128).astype(BF16)
 
-        def send_rows(i, _):
+        for i in range(count * 6):
             cc, t = first + i // 6, i % 6
             dst = col_of(block_y(cc), t)
-            mine = dst == me_c
-
-            @pl.when(jnp.logical_not(mine))
-            def _():
+
+            def start():
                 pltpu.make_async_remote_copy(
                     wmsg.at[cc * 6 + t], wrecv.at[me_c], w_send, w_recv,
                     device_id=(me_r, dst), device_id_type=MESH,
                 ).start()
 
+            if cc < 3:
+                start()
+                continue
+            mine = dst == me_c
+            pl.when(jnp.logical_not(mine))(start)
+
             @pl.when(mine)
             def _():
                 pltpu.make_async_copy(wmsg.at[cc * 6 + t], wrecv.at[me_c], w_recv).start()
 
-            return 0
-
-        lax.fori_loop(0, count * 6, send_rows, 0)
-
-    attend(0, 2)
-    pair_steps(4, 0)
-    attend(2, 1)
-    stage_hidden(11, 1)
-    stage_mid(10, 0)
-    stage_bias(9, 1)
-    stage_mid(11, 1)
-    stage_bias(10, 0)
-    stage_bias(11, 1)
-    mid_out(10).start()
-    mid_out(11).start()
+    attend(0, 3)
+    pair_copy(11).wait()
+    stage_hidden(10, 1)
+    stage_norm(11, 2)
+    stage_mid(0)
+    stage_hidden(11, 2)
+    stage_mid(1)
+    stage_mid(2)
+    stage_bias(3)
+    for k in range(9, 12):
+        mid_out(k).start()
     attend(3, 1)
 
     @pl.when(is_owner)
     def _():
-        pick = jnp.where(iota((8, 256), 1) == own_o * 8 + iota((8, 256), 0), 1.0, 0.0).astype(BF16)
-        resid = nt(pick, sqk[...])
+        resid = raw_v[pl.ds(pl.multiple_of(own_o * 8, 8), 8), :]
         c_out.wait()
         c_proj.wait()
         pltpu.make_async_copy(wrecv, wrecv, w_recv).wait()
@@ -373,31 +354,25 @@
             emsg[c, 0] = left
             emsg[c, 1] = tile.astype(BF16)
 
-        def send_right(r, _):
+        slot = lax.rem(own_o, 6)
+        for r in range(R_DEV):
             here = jnp.logical_and(r == me_r, dest_c == me_c)
 
             @pl.when(jnp.logical_not(here))
             def _():
                 pltpu.make_async_remote_copy(
-                    rmsg, rrecv.at[own_o % 6], r_send, r_recv, device_id=(r, dest_c), device_id_type=MESH
+                    rmsg, rrecv.at[slot], r_send, r_recv, device_id=(r, dest_c), device_id_type=MESH
                 ).start()
 
             @pl.when(here)
             def _():
-                pltpu.make_async_copy(rmsg, rrecv.at[own_o % 6], r_recv).start()
-
-            return 0
-
-        lax.fori_loop(0, R_DEV, send_right, 0)
-
-        def send_left(s, _):
-            dst = (me_c + s) % C_DEV
+                pltpu.make_async_copy(rmsg, rrecv.at[slot], r_recv).start()
+
+        for s in range(1, C_DEV):
+            dst = lax.rem(me_c + (s + 15) % 31 + 1, C_DEV)
             pltpu.make_async_remote_copy(
                 emsg.at[dst], erecv.at[own_o], e_send, e_recv, device_id=(me_r, dst), device_id_type=MESH
             ).start()
-            return 0
-
-        lax.fori_loop(1, C_DEV, send_left, 0)
         pltpu.make_async_copy(emsg.at[me_c], erecv.at[own_o], e_recv).start()
 
     @pl.when(jnp.logical_not(is_owner))
@@ -409,7 +384,7 @@
     pltpu.make_async_copy(msgs.at[0 : C_DEV - 1], msgs.at[0 : C_DEV - 1], s_send).wait()
 
     def sent_rows(i, _):
-        @pl.when(col_of(block_y(i // 6), i % 6) != me_c)
+        @pl.when(col_of(block_y(lax.div(i, 6)), lax.rem(i, 6)) != me_c)
         def _():
             pltpu.make_async_copy(wmsg.at[i], wmsg.at[i], w_send).wait()
 
@@ -438,7 +413,10 @@
         lax.fori_loop(0, R_DEV, sent_right, 0)
 
 
-def pair_kernel(mid_h, left_ref, right_ref, wpair_ref, out_h, mid_v, out_v, in_sem, out_sem):
+def pair_kernel(
+    mid_h, left_h, right_h, wpair_h, seqt_h, out_h, seq_o,
+    left_ref, right_ref, wpair_ref, seq_v, mid_v, out_v, small_sem, in_sem, out_sem,
+):
     n = NI // KSTEPS
 
     def rows(k):
@@ -450,8 +428,20 @@
     def put(k):
         return pltpu.make_async_copy(out_v.at[rows(k)], out_h.at[rows(k)], out_sem)
 
+    small = [
+        pltpu.make_async_copy(left_h, left_ref, small_sem.at[0]),
+        pltpu.make_async_copy(right_h, right_ref, small_sem.at[1]),
+        pltpu.make_async_copy(wpair_h, wpair_ref, small_sem.at[2]),
+        pltpu.make_async_copy(seqt_h, seq_v, small_sem.at[3]),
+    ]
+    for cp in small:
+        cp.start()
     for k in range(KSTEPS):
         fetch(k).start()
+    for cp in small:
+        cp.wait()
+    seq_put = pltpu.make_async_copy(seq_v, seq_o, small_sem.at[0])
+    seq_put.start()
     lane = iota((NJ, C), 1)
     right = right_ref[...]
     scale = jnp.where(lane < 64, right, 1.0)
@@ -468,6 +458,7 @@
         return 0
 
     lax.fori_loop(0, KSTEPS, step, 0)
+    seq_put.wait()
     pltpu.make_async_copy(out_v, out_h, out_sem).wait()
 
 
@@ -492,8 +483,9 @@
             pltpu.VMEM((RC * NJ, C), BF16),
             pltpu.VMEM((RC * NJ, C), BF16),
             pltpu.VMEM((RC * NJ, C), BF16),
-            pltpu.VMEM((RC * NJ, C), F32),
-            pltpu.VMEM((RC * NJ, C), F32),
+            pltpu.VMEM((RC * NJ, C), BF16),
+            pltpu.VMEM((RC * NJ, C), BF16),
+            pltpu.VMEM((BLK * NJ, C), F32),
             pltpu.VMEM((2, 6, NI, 128), F32),
             pltpu.VMEM((8 * C, 256), BF16),
             pltpu.VMEM((32, R_DEV * NI), BF16),
@@ -507,7 +499,8 @@
             pltpu.VMEM((D, C), BF16),
             pltpu.VMEM((C_DEV, 32, 256), BF16),
             pltpu.VMEM((D, 256), BF16),
-            pltpu.VMEM((D, 256), BF16),
+            pltpu.VMEM((256, D), F32),
+            pltpu.VMEM((256, D), BF16),
             pltpu.VMEM((NI, D), BF16),
             pltpu.VMEM((NJ, 2 * D), F32),
             pltpu.VMEM((2, 16 * NJ, 512), BF16),
@@ -529,21 +522,26 @@
         ),
         name="trunk_main",
     )(pair, seq.T, w_hidden, w_back, w_bias.T, w_query, w_key, w_value, w_out, w_project)
-    pair_out = pl.pallas_call(
+    pair_out, seq_out = pl.pallas_call(
         pair_kernel,
-        out_shape=jax.ShapeDtypeStruct((NI, NJ, C), BF16),
-        in_specs=[hbm, vmem, vmem, vmem],
-        out_specs=hbm,
+        out_shape=(jax.ShapeDtypeStruct((NI, NJ, C), BF16), jax.ShapeDtypeStruct((32, NI), BF16)),
+        in_specs=[hbm] * 5,
+        out_specs=(hbm, hbm),
         scratch_shapes=[
+            pltpu.VMEM((NI, 128), F32),
+            pltpu.VMEM((NJ, 128), F32),
+            pltpu.VMEM((C, C), BF16),
+            pltpu.VMEM((32, NI), BF16),
             pltpu.VMEM((NI, NJ, C), BF16),
             pltpu.VMEM((NI, NJ, C), BF16),
+            dma((4,)),
             dma((KSTEPS,)),
             dma,
         ],
-        compiler_params=pltpu.CompilerParams(vmem_limit_bytes=16 * 1024 * 1024),
+        compiler_params=pltpu.CompilerParams(vmem_limit_bytes=60 * 1024 * 1024),
         name="pair_update",
-    )(mid, left, right, w_pair)
-    return pair_out, seq_new.T
+    )(mid, left, right, w_pair, seq_new)
+    return pair_out, seq_out.T
 
 
 def solution(mesh):

time: 53.7 us -> 44.9 us (0.84)
  Pallas kernels: 48.5 us -> 43.8 us
  local copies, waits for them, and re-layouts: 3.9 us -> 0 us
    unnamed x11 -> x0, local copies, waits for them, and re-layouts: 3.9 us -> none
    pallas_call x1, Pallas kernels: 6.22 us -> 3.52 us  [local(): pl.pallas_call(pair_kernel, out_shape=(jax.ShapeDtypeStruct((NI, NJ, C),...]
    pallas_call x1, Pallas kernels: 42.3 us -> 40.3 us  [local(): pl.pallas_call(main_kernel, out_shape=(jax.ShapeDtypeStruct((NI, NJ, C),...]
where the time goes in v3:
time: 44.9 us; the launch traced here: 44.4 us
  Pallas kernels  43.8 us (98%)
  between operations  0.64 us (1%)
    pallas_call x1, Pallas kernels, local(): pl.pallas_call(main_kernel, out_shape=(jax.ShapeDtypeStruct((NI, NJ, C),...  40.3 us
    pallas_call x1, Pallas kernels, local(): pl.pallas_call(pair_kernel, out_shape=(jax.ShapeDtypeStruct((NI, NJ, C),...  3.52 us

profile of v3, /device:TPU:1, one launch (start us, length us, event | category | flops | bytes accessed | tf_op | source)
XLA Modules:
  0.0 44.4 jit_solution(613591339970766884)
XLA Ops:
  0.6 40.3 %trunk_main.1 = (bf16[192,48,128]{2,1,0:T(8,128)(2,1)}, f32[192,128]{1,0:T(8,128)}, f32[48,128]{1,0:T(8,128)}, bf16[32,192]{1,0:T(8,128)(2,1)}) custom-call(bf16[192,48,128]{2,1,0:T(8,128)(2,1)} %pair_h.1, bf16[32,1536]{1,0:T(8,128)(2,1)} %bitcast.3, bf16[128,512]{1,0:T(8,128)(2,1)} %whid_h.1, bf16[512,128]{1,0:T(8,128)(2,1)} %wback_h.1, ...), custom_call_target="tpu_custom_call" | custom-call | tf_op jit(solution)/shard_map/trunk_main/pallas_call | solution.py:469
  40.9 3.5 %pair_update.1 = (bf16[192,48,128]{2,1,0:T(8,128)(2,1)}, bf16[32,192]{1,0:T(8,128)(2,1)}) custom-call(bf16[192,48,128]{2,1,0:T(8,128)(2,1)} %get-tuple-element.8.mid_h, f32[192,128]{1,0:T(8,128)} %get-tuple-element.9.left_h, f32[48,128]{1,0:T(8,128)} %get-tuple-element.10.right_h, bf16[128,128]{1,0:T(8,128)(2,1)} %wpair_h.1, ...), custom_call_target="tpu_custom_call" | custom-call | tf_op jit(solution)/shard_map/pair_update/pallas_call | solution.py:525

commit v4 on v3

--- a/solution.py
+++ b/solution.py
@@ -21,6 +21,7 @@
 BLK = 48
 SPB = BLK // RC
 KSTEPS = 4
+KROWS = NI // KSTEPS
 SCALE = 32 ** (-0.5)
 MESH = pl.DeviceIdType.MESH
 
@@ -44,6 +45,18 @@
     return cen * lax.rsqrt(var + EPS)
 
 
+def row_sum(x):
+    parts = [x[:, t : t + 128] for t in range(0, D, 128)]
+    while len(parts) > 1:
+        parts = [a + b for a, b in zip(parts[0::2], parts[1::2])]
+    return jnp.sum(parts[0], axis=-1, keepdims=True)
+
+
+def wide_norm(x):
+    cen = x - row_sum(x) * (1.0 / D)
+    return cen * lax.rsqrt(row_sum(cen * cen) * (1.0 / D) + EPS)
+
+
 def iota(shape, dim):
     return lax.broadcasted_iota(jnp.int32, shape, dim)
 
@@ -62,11 +75,11 @@
 
 def main_kernel(
     pair_h, seq_h, whid_h, wback_h, wbias_h, wq_h, wk_h, wv_h, wout_h, wproj_h,
-    mid_h, left_o, right_o, seq_o,
+    mid_h, left_o, right_o,
     pair_v, mid_v, nb0, nb1, nb2, mb0, mb1, mb2, mn_v, bias_v, bmat_v,
     seq_v, whid_v, wback_v, wbias_v, wq_v, wk_v, wv_v, wout_v, wproj_v,
-    msgs, sqk, raw_v, sqn, q_v, kv_v, kbd, vbd, w_v, expand_v, wmsg, wrecv, emsg, erecv, rmsg, rrecv,
-    in_sem, pin_sem, mid_sem, s_send, s_recv, w_send, w_recv, e_send, e_recv, r_send, r_recv,
+    own0_v, msgs, sqk0, sqk1, raw_v, sqn, q_v, kv_v, kbd, vbd, w_v, expand_v, wmsg, wrecv, emsg, erecv, rmsg, rrecv,
+    in_sem, pin_sem, mid_sem, s0_send, s0_recv, s1_send, s1_recv, w_send, w_recv, e_send, e_recv, r_send, r_recv,
 ):
     me_r, me_c = lax.axis_index("row"), lax.axis_index("col")
     own_o, is_owner, me_y = owner_of(me_c)
@@ -123,7 +136,8 @@
     base = pl.multiple_of((me_r * 3 // 2) * 128, 128)
     own = seq_v[:, pl.ds(base, 256)].astype(F32)
     own = jnp.where(me_r % 2 == 1, pltpu.roll(own, 192, 1), own)
-    own0, own1 = own[:, 0:128].astype(BF16), own[:, 128:256]
+    own0_v[...] = own[:, 0:128].astype(BF16)
+    own1 = own[:, 128:256]
     for c in range(C_DEV):
         t, o = (c * NJ) // 128, (c * NJ) % 128
         keys = seq_v[:, t * 128 : t * 128 + 128].astype(F32)
@@ -131,8 +145,24 @@
             keys = jnp.where(lane32 >= o, keys, seq_v[:, t * 128 + 128 : t * 128 + 256].astype(F32))
         if o != 64:
             keys = pltpu.roll(keys, (64 - o) % 128, 1)
-        msgs[c, :, 0:128] = own0
-        msgs[c, :, 128:256] = jnp.where(lane32 < 64, own1, jnp.where(lane32 < 112, keys, 0.0)).astype(BF16)
+        msgs[c] = jnp.where(lane32 < 64, own1, jnp.where(lane32 < 112, keys, 0.0)).astype(BF16)
+
+    pl.semaphore_wait(
+        barrier, C_DEV - 1 + jnp.where(is_owner, R_DEV, 0) - jnp.where(self_right, 1, 0)
+    )
+    my_slab = pl.ds(pl.multiple_of(me_c * 32, 32), 32)
+    for s in range(1, C_DEV):
+        dst = lax.rem(me_c + s, C_DEV)
+        pltpu.make_async_remote_copy(
+            msgs.at[dst], sqk1.at[my_slab], s1_send, s1_recv, device_id=(me_r, dst), device_id_type=MESH
+        ).start()
+    for s in range(1, C_DEV):
+        dst = lax.rem(me_c + s, C_DEV)
+        pltpu.make_async_remote_copy(
+            own0_v, sqk0.at[my_slab], s0_send, s0_recv, device_id=(me_r, dst), device_id_type=MESH
+        ).start()
+    pltpu.make_async_copy(msgs.at[me_c], sqk1.at[my_slab], s1_recv).start()
+    pltpu.make_async_copy(own0_v, sqk0.at[my_slab], s0_recv).start()
 
     c_bias.wait()
     spread = jnp.where(
@@ -187,15 +217,20 @@
     def mid_out(k):
         return pltpu.make_async_copy(mid_v.at[rows_of(k)], mid_h.at[true_rows(k)], mid_sem)
 
-    def pair_block(t, _):
+    def pair_block(t, _, first=False):
         for u in range(3):
             pair_copy(3 * t + 2 + u).wait()
+        if first:
+            stage_norm(0, 0)
+            stage_hidden(0, 0)
+            stage_norm(1, 1)
+        else:
+            stage_bias(t - 1)
         for u in range(3):
             k, s = 3 * t + 1 + u, (1 + u) % 3
             stage_hidden(k, s)
             stage_norm(k + 1, (s + 1) % 3)
             stage_mid(u)
-        stage_bias(t)
         for u in range(3):
             mid_out(3 * t + u).start()
         return 0
@@ -204,35 +239,21 @@
     c_back.wait()
     pair_copy(0).wait()
     pair_copy(1).wait()
-    pl.semaphore_wait(
-        barrier, C_DEV - 1 + jnp.where(is_owner, R_DEV, 0) - jnp.where(self_right, 1, 0)
-    )
-    my_slab = pl.ds(pl.multiple_of(me_c * 32, 32), 32)
-    for s in range(1, C_DEV):
-        dst = lax.rem(me_c + s, C_DEV)
-        pltpu.make_async_remote_copy(
-            msgs.at[dst], sqk.at[my_slab], s_send, s_recv, device_id=(me_r, dst), device_id_type=MESH
-        ).start()
-    pltpu.make_async_copy(msgs.at[me_c], sqk.at[my_slab], s_recv).start()
-    stage_norm(0, 0)
-    stage_hidden(0, 0)
-    stage_norm(1, 1)
-
-    lax.fori_loop(0, 3, pair_block, 0)
-
-    pltpu.make_async_copy(sqk, sqk, s_recv).wait()
-    ident = jnp.where(iota((256, 256), 0) == iota((256, 256), 1), 1.0, 0.0).astype(BF16)
-    raw_v[...] = nt(ident, sqk[...])
+    pair_block(0, 0, first=True)
+    lax.fori_loop(1, 3, pair_block, 0)
+    stage_bias(2)
+
+    ident = jnp.where(iota((128, 128), 0) == iota((128, 128), 1), 1.0, 0.0).astype(BF16)
 
     def norm_rows(k, _):
         for u in range(4):
             rows = pl.ds(pl.multiple_of(k * 64 + u * 16, 16), 16)
-            sqn[rows, :] = layer_norm(raw_v[rows, :]).astype(BF16)
+            sqn[rows, :] = wide_norm(raw_v[rows, :]).astype(BF16)
         return 0
 
-    lax.fori_loop(0, 4, norm_rows, 0)
-    c_q.wait()
-    q_v[...] = nn(sqn[:NI], wq_v[...]).astype(BF16)
+    pltpu.make_async_copy(sqk1, sqk1, s1_recv).wait()
+    raw_v[128:256] = nt(ident, sqk1[...])
+    lax.fori_loop(2, 4, norm_rows, 0)
     c_k.wait()
     c_v.wait()
     kv_v[:, 0:D] = nn(sqn[NI : NI + NJ], wk_v[...])
@@ -251,6 +272,11 @@
         return 0
 
     lax.fori_loop(0, NJ // 4, spread_keys, 0)
+    pltpu.make_async_copy(sqk0, sqk0, s0_recv).wait()
+    raw_v[0:128] = nt(ident, sqk0[...])
+    lax.fori_loop(0, 2, norm_rows, 0)
+    c_q.wait()
+    q_v[...] = nn(sqn[:NI], wq_v[...]).astype(BF16)
 
     def attend(first, count):
         n = count * BLK
@@ -341,18 +367,16 @@
         wide = nn(jnp.concatenate([high, low], axis=1), expand_v[...]).reshape(C_DEV, OWN, D)
         attended = jnp.sum(wide * wrecv[:, :, 0:D].astype(F32), axis=0).astype(BF16)
         seq_new = (resid + nn(attended, wout_v[...])).astype(BF16).astype(F32)
-        proj = nn(layer_norm(seq_new).astype(BF16), wproj_v[...]).astype(BF16).astype(F32)
+        proj = nn(wide_norm(seq_new).astype(BF16), wproj_v[...]).astype(BF16).astype(F32)
         turned = pltpu.roll(proj, 64, 1)
         lane8 = iota((OWN, 128), 1)
-        left = jnp.where(lane8 < 64, proj, turned).astype(BF16)
         right = jnp.where(lane8 < 64, turned, proj).astype(BF16)
         rmsg[...] = right
         for c in range(C_DEV):
             tile = seq_new[:, (c // 4) * 128 : (c // 4) * 128 + 128]
-            if c % 4:
-                tile = pltpu.roll(tile, 128 - 32 * (c % 4), 1)
-            emsg[c, 0] = left
-            emsg[c, 1] = tile.astype(BF16)
+            if c % 4 != 2:
+                tile = pltpu.roll(tile, (192 - 32 * (c % 4)) % 128, 1)
+            emsg[c] = jnp.where(lane8 < 64, proj, tile).astype(BF16)
 
         slot = lax.rem(own_o, 6)
         for r in range(R_DEV):
@@ -381,7 +405,9 @@
         c_proj.wait()
 
     pltpu.make_async_copy(mid_v, mid_h, mid_sem).wait()
-    pltpu.make_async_copy(msgs.at[0 : C_DEV - 1], msgs.at[0 : C_DEV - 1], s_send).wait()
+    pltpu.make_async_copy(msgs.at[0 : C_DEV - 1], msgs.at[0 : C_DEV - 1], s1_send).wait()
+    others = pl.ds(0, 32 * (C_DEV - 1))
+    pltpu.make_async_copy(sqk0.at[others], sqk0.at[others], s0_send).wait()
 
     def sent_rows(i, _):
         @pl.when(col_of(block_y(lax.div(i, 6)), lax.rem(i, 6)) != me_c)
@@ -393,11 +419,11 @@
     lax.fori_loop(0, OWNERS, sent_rows, 0)
 
     pltpu.make_async_copy(rrecv, rrecv, r_recv).wait()
-    right_o[...] = rrecv[...].astype(F32).reshape(NJ, 128)
+    right_put = pltpu.make_async_copy(rrecv, right_o, in_sem.at[0])
+    right_put.start()
     pltpu.make_async_copy(erecv, erecv, e_recv).wait()
-    left_o[...] = erecv[:, 0].astype(F32).reshape(NI, 128)
-    eye = jnp.where(iota((32, 128), 0) == iota((32, 128), 1), 1.0, 0.0).astype(BF16)
-    seq_o[...] = nt(eye, erecv[:, 1].astype(F32).reshape(NI, 128).astype(BF16)).astype(BF16)
+    left_put = pltpu.make_async_copy(erecv, left_o, in_sem.at[1])
+    left_put.start()
 
     @pl.when(is_owner)
     def _():
@@ -411,50 +437,46 @@
             return 0
 
         lax.fori_loop(0, R_DEV, sent_right, 0)
+    right_put.wait()
+    left_put.wait()
 
 
 def pair_kernel(
-    mid_h, left_h, right_h, wpair_h, seqt_h, out_h, seq_o,
-    left_ref, right_ref, wpair_ref, seq_v, mid_v, out_v, small_sem, in_sem, out_sem,
+    mid_h, left_h, right_h, wpair_h, out_h, seq_h,
+    left_b, right_b, wpair_v, left_v, seq_v, mid_v, out_v, small_sem, in_sem, out_sem,
 ):
-    n = NI // KSTEPS
-
-    def rows(k):
-        return pl.ds(pl.multiple_of(k * n, n), n)
-
-    def fetch(k):
-        return pltpu.make_async_copy(mid_h.at[rows(k)], mid_v.at[rows(k)], in_sem.at[k])
-
-    def put(k):
-        return pltpu.make_async_copy(out_v.at[rows(k)], out_h.at[rows(k)], out_sem)
-
+    spans = [pl.ds(k * KROWS, KROWS) for k in range(KSTEPS)]
     small = [
-        pltpu.make_async_copy(left_h, left_ref, small_sem.at[0]),
-        pltpu.make_async_copy(right_h, right_ref, small_sem.at[1]),
-        pltpu.make_async_copy(wpair_h, wpair_ref, small_sem.at[2]),
-        pltpu.make_async_copy(seqt_h, seq_v, small_sem.at[3]),
+        pltpu.make_async_copy(src, dst, small_sem.at[k])
+        for k, (src, dst) in enumerate(((left_h, left_b), (right_h, right_b), (wpair_h, wpair_v)))
     ]
     for cp in small:
         cp.start()
-    for k in range(KSTEPS):
-        fetch(k).start()
+    fetches = [pltpu.make_async_copy(mid_h.at[r], mid_v.at[r], in_sem.at[k]) for k, r in enumerate(spans)]
+    for cp in fetches:
+        cp.start()
     for cp in small:
         cp.wait()
-    seq_put = pltpu.make_async_copy(seq_v, seq_o, small_sem.at[0])
-    seq_put.start()
     lane = iota((NJ, C), 1)
-    right = right_ref[...]
+    right = right_b[...].astype(F32).reshape(NJ, C)
     scale = jnp.where(lane < 64, right, 1.0)
     shift = jnp.where(lane < 64, 0.0, -right)
+    arrived = left_b[...].astype(F32).reshape(NI, C)
+    left_v[...] = jnp.where(iota((NI, C), 1) < 64, arrived, pltpu.roll(arrived, 64, 1))
+    pick = jnp.where(iota((32, C), 1) == iota((32, C), 0) + 64, 1.0, 0.0).astype(BF16)
+    seq_v[...] = nt(pick, left_b[...].reshape(NI, C)).astype(BF16)
+    seq_put = pltpu.make_async_copy(seq_v, seq_h, small_sem.at[0])
+    seq_put.start()
 
     def step(k, _):
-        fetch(k).wait()
-        left = left_ref[rows(k), :].reshape(n, 1, C)
-        feature = (left * scale[None] + shift[None]).astype(BF16).reshape(n * NJ, C)
-        update = nn(feature, wpair_ref[...])
-        mid = mid_v[rows(k)].astype(F32).reshape(n * NJ, C)
-        out_v[rows(k)] = (mid + update).astype(BF16).reshape(n, NJ, C)
-        put(k).start()
+        rows = pl.ds(pl.multiple_of(k * KROWS, KROWS), KROWS)
+        pltpu.make_async_copy(mid_h.at[rows], mid_v.at[rows], in_sem.at[k]).wait()
+        left = left_v[rows, :].reshape(KROWS, 1, C)
+        feature = (left * scale[None] + shift[None]).astype(BF16).reshape(KROWS * NJ, C)
+        update = nn(feature, wpair_v[...])
+        mid = mid_v[rows].astype(F32).reshape(KROWS * NJ, C)
+        out_v[rows] = (mid + update).astype(BF16).reshape(KROWS, NJ, C)
+        pltpu.make_async_copy(out_v.at[rows], out_h.at[rows], out_sem).start()
         return 0
 
     lax.fori_loop(0, KSTEPS, step, 0)
@@ -464,18 +486,16 @@
 
 def local(pair, seq, w_hidden, w_back, w_bias, w_query, w_key, w_value, w_out, w_project, w_pair):
     hbm = pl.BlockSpec(memory_space=pl.ANY)
-    vmem = pl.BlockSpec(memory_space=pltpu.VMEM)
     dma = pltpu.SemaphoreType.DMA
-    mid, left, right, seq_new = pl.pallas_call(
+    mid, left, right = pl.pallas_call(
         main_kernel,
         out_shape=(
             jax.ShapeDtypeStruct((NI, NJ, C), BF16),
-            jax.ShapeDtypeStruct((NI, 128), F32),
-            jax.ShapeDtypeStruct((NJ, 128), F32),
-            jax.ShapeDtypeStruct((32, NI), BF16),
+            jax.ShapeDtypeStruct((OWNERS, OWN, 128), BF16),
+            jax.ShapeDtypeStruct((6, OWN, 128), BF16),
         ),
         in_specs=[hbm] * 10,
-        out_specs=(hbm, vmem, vmem, vmem),
+        out_specs=(hbm, hbm, hbm),
         scratch_shapes=[
             pltpu.VMEM((NI, NJ, C), BF16),
             pltpu.VMEM((NI, NJ, C), BF16),
@@ -497,8 +517,10 @@
             pltpu.VMEM((D, D), BF16),
             pltpu.VMEM((D, D), BF16),
             pltpu.VMEM((D, C), BF16),
-            pltpu.VMEM((C_DEV, 32, 256), BF16),
-            pltpu.VMEM((D, 256), BF16),
+            pltpu.VMEM((32, 128), BF16),
+            pltpu.VMEM((C_DEV, 32, 128), BF16),
+            pltpu.VMEM((D, 128), BF16),
+            pltpu.VMEM((D, 128), BF16),
             pltpu.VMEM((256, D), F32),
             pltpu.VMEM((256, D), BF16),
             pltpu.VMEM((NI, D), BF16),
@@ -509,13 +531,13 @@
             pltpu.VMEM((256, D), BF16),
             pltpu.VMEM((OWNERS, OWN, WL), BF16),
             pltpu.VMEM((C_DEV, OWN, WL), BF16),
-            pltpu.VMEM((C_DEV, 2, OWN, 128), BF16),
-            pltpu.VMEM((OWNERS, 2, OWN, 128), BF16),
+            pltpu.VMEM((C_DEV, OWN, 128), BF16),
+            pltpu.VMEM((OWNERS, OWN, 128), BF16),
             pltpu.VMEM((OWN, 128), BF16),
             pltpu.VMEM((6, OWN, 128), BF16),
             dma((9,)),
             dma((STEPS,)),
-            dma, dma, dma, dma, dma, dma, dma, dma, dma,
+            dma, dma, dma, dma, dma, dma, dma, dma, dma, dma, dma,
         ],
         compiler_params=pltpu.CompilerParams(
             collective_id=0, has_side_effects=True, vmem_limit_bytes=60 * 1024 * 1024
@@ -525,22 +547,23 @@
     pair_out, seq_out = pl.pallas_call(
         pair_kernel,
         out_shape=(jax.ShapeDtypeStruct((NI, NJ, C), BF16), jax.ShapeDtypeStruct((32, NI), BF16)),
-        in_specs=[hbm] * 5,
+        in_specs=[hbm] * 4,
         out_specs=(hbm, hbm),
         scratch_shapes=[
+            pltpu.VMEM((OWNERS, OWN, 128), BF16),
+            pltpu.VMEM((6, OWN, 128), BF16),
+            pltpu.VMEM((C, C), BF16),
             pltpu.VMEM((NI, 128), F32),
-            pltpu.VMEM((NJ, 128), F32),
-            pltpu.VMEM((C, C), BF16),
             pltpu.VMEM((32, NI), BF16),
             pltpu.VMEM((NI, NJ, C), BF16),
             pltpu.VMEM((NI, NJ, C), BF16),
-            dma((4,)),
+            dma((3,)),
             dma((KSTEPS,)),
             dma,
         ],
         compiler_params=pltpu.CompilerParams(vmem_limit_bytes=60 * 1024 * 1024),
         name="pair_update",
-    )(mid, left, right, w_pair, seq_new)
+    )(mid, left, right, w_pair)
     return pair_out, seq_out.T
 
 

time: 44.9 us -> 43.4 us (0.967)
  Pallas kernels: 43.8 us -> 42.1 us
    pallas_call x1, Pallas kernels: 40.3 us -> 38.4 us  [local(): pl.pallas_call(main_kernel, out_shape=(jax.ShapeDtypeStruct((NI, NJ, C),...]
where the time goes in v4:
time: 43.4 us; the launch traced here: 42.7 us
  Pallas kernels  42.1 us (97%)
  between operations  0.64 us (1%)
    pallas_call x1, Pallas kernels, local(): pl.pallas_call(main_kernel, out_shape=(jax.ShapeDtypeStruct((NI, NJ, C),...  38.4 us
    pallas_call x1, Pallas kernels, local(): pl.pallas_call(pair_kernel, out_shape=(jax.ShapeDtypeStruct((NI, NJ, C),...  3.67 us

profile of v4, /device:TPU:1, one launch (start us, length us, event | category | flops | bytes accessed | tf_op | source)
XLA Modules:
  0.0 42.7 jit_solution(10469112078993581007)
XLA Ops:
  0.6 38.4 %trunk_main.1 = (bf16[192,48,128]{2,1,0:T(8,128)(2,1)}, bf16[24,8,128]{2,1,0:T(8,128)(2,1)}, bf16[6,8,128]{2,1,0:T(8,128)(2,1)}) custom-call(bf16[192,48,128]{2,1,0:T(8,128)(2,1)} %pair_h.1, bf16[32,1536]{1,0:T(8,128)(2,1)} %bitcast.3, bf16[128,512]{1,0:T(8,128)(2,1)} %whid_h.1, bf16[512,128]{1,0:T(8,128)(2,1)} %wback_h.1, bf16[32,128]{1,0:T(8,128)(2,1)} %bitcast.4, ...), custom_call_target="tpu_custom_call" | custom-call | tf_op jit(solution)/shard_map/trunk_main/pallas_call | solution.py:490
  39.1 3.7 %pair_update.1 = (bf16[192,48,128]{2,1,0:T(8,128)(2,1)}, bf16[32,192]{1,0:T(8,128)(2,1)}) custom-call(bf16[192,48,128]{2,1,0:T(8,128)(2,1)} %get-tuple-element.7.mid_h, bf16[24,8,128]{2,1,0:T(8,128)(2,1)} %get-tuple-element.8.left_h, bf16[6,8,128]{2,1,0:T(8,128)(2,1)} %get-tuple-element.9.right_h, bf16[128,128]{1,0:T(8,128)(2,1)} %wpair_h.1), custom_call_target="tpu_custom_call" | custom-call | tf_op jit(solution)/shard_map/pair_update/pallas_call | solution.py:547

commit v5 on v4

--- a/solution.py
+++ b/solution.py
@@ -15,7 +15,6 @@
 R_DEV, C_DEV = 8, 32
 NI, NJ, C, D, PH = 192, 48, 128, 1024, 512
 OWNERS, OWN = 24, 8
-WL = D + 128
 RC = 16
 STEPS = NI // RC
 BLK = 48
@@ -78,8 +77,8 @@
     mid_h, left_o, right_o,
     pair_v, mid_v, nb0, nb1, nb2, mb0, mb1, mb2, mn_v, bias_v, bmat_v,
     seq_v, whid_v, wback_v, wbias_v, wq_v, wk_v, wv_v, wout_v, wproj_v,
-    own0_v, msgs, sqk0, sqk1, raw_v, sqn, q_v, kv_v, kbd, vbd, w_v, expand_v, wmsg, wrecv, emsg, erecv, rmsg, rrecv,
-    in_sem, pin_sem, mid_sem, s0_send, s0_recv, s1_send, s1_recv, w_send, w_recv, e_send, e_recv, r_send, r_recv,
+    own0_v, msgs, sqk0, sqk1, raw_v, sqn, q_v, kv_v, kbd, vbd, w_v, expand_v, fac2_v, wmsg0, wmsg1, wrecv0, wrecv1, emsg, erecv, rmsg, rrecv,
+    in_sem, pin_sem, mid_sem, s0_send, s0_recv, s1_send, s1_recv, w0_send, w0_recv, w1_send, w1_recv, e_send, e_recv, r_send, r_recv,
 ):
     me_r, me_c = lax.axis_index("row"), lax.axis_index("col")
     own_o, is_owner, me_y = owner_of(me_c)
@@ -300,10 +299,6 @@
                 total = w if total is None else total + w
             for shift in (16, 32, 64):
                 total = total + pltpu.roll(total, shift, 1)
-            weighted = nn(w_v[g, here, :], vbd[g])
-            wmsg[first * 6 : (first + count) * 6, :, g * 512 : (g + 1) * 512] = weighted.reshape(
-                count * 6, OWN, 512
-            ).astype(BF16)
             high = top.astype(BF16).astype(F32)
             middle = (top - high).astype(BF16).astype(F32)
             low = (top - high) - middle
@@ -312,28 +307,26 @@
         for p in range(4):
             for g in range(2):
                 stats = jnp.where(lane // 16 == p * 2 + g, parts[g][p], stats)
-        wmsg[first * 6 : (first + count) * 6, :, D:WL] = stats.reshape(count * 6, OWN, 128).astype(BF16)
-
-        for i in range(count * 6):
-            cc, t = first + i // 6, i % 6
-            dst = col_of(block_y(cc), t)
-
-            def start():
-                pltpu.make_async_remote_copy(
-                    wmsg.at[cc * 6 + t], wrecv.at[me_c], w_send, w_recv,
-                    device_id=(me_r, dst), device_id_type=MESH,
-                ).start()
-
-            if cc < 3:
+        slots = slice(first * 6, (first + count) * 6)
+        for g in range(2):
+            msg, land, ssem, rsem = (
+                (wmsg0, wrecv0, w0_send, w0_recv), (wmsg1, wrecv1, w1_send, w1_recv)
+            )[g]
+            weighted = nn(w_v[g, here, :], vbd[g])
+            msg[slots, :, 0:512] = weighted.reshape(count * 6, OWN, 512).astype(BF16)
+            if g == 0:
+                msg[slots, :, 512:640] = stats.reshape(count * 6, OWN, 128).astype(BF16)
+            for i in range(count * 6 if first < 3 else 0):
+                cc, t = first + i // 6, i % 6
+                dst = col_of(block_y(cc), t)
+
+                def start():
+                    pltpu.make_async_remote_copy(
+                        msg.at[cc * 6 + t], land.at[me_c], ssem, rsem,
+                        device_id=(me_r, dst), device_id_type=MESH,
+                    ).start()
+
                 start()
-                continue
-            mine = dst == me_c
-            pl.when(jnp.logical_not(mine))(start)
-
-            @pl.when(mine)
-            def _():
-                pltpu.make_async_copy(wmsg.at[cc * 6 + t], wrecv.at[me_c], w_recv).start()
-
     attend(0, 3)
     pair_copy(11).wait()
     stage_hidden(10, 1)
@@ -346,14 +339,30 @@
     for k in range(9, 12):
         mid_out(k).start()
     attend(3, 1)
+    for t in range(6):
+        dst = col_of(block_y(3), t)
+        halves = ((wmsg0, wrecv0, w0_send, w0_recv), (wmsg1, wrecv1, w1_send, w1_recv))
+
+        @pl.when(dst != me_c)
+        def _():
+            for msg, land, ssem, rsem in halves:
+                pltpu.make_async_remote_copy(
+                    msg.at[18 + t], land.at[me_c], ssem, rsem, device_id=(me_r, dst), device_id_type=MESH
+                ).start()
+
+        @pl.when(dst == me_c)
+        def _():
+            for msg, land, _ssem, rsem in halves:
+                pltpu.make_async_copy(msg.at[18 + t], land.at[me_c], rsem).start()
+
 
     @pl.when(is_owner)
     def _():
         resid = raw_v[pl.ds(pl.multiple_of(own_o * 8, 8), 8), :]
         c_out.wait()
         c_proj.wait()
-        pltpu.make_async_copy(wrecv, wrecv, w_recv).wait()
-        st = wrecv[:, :, D:WL].astype(F32).reshape(C_DEV * OWN, 128)
+        pltpu.make_async_copy(wrecv0, wrecv0, w0_recv).wait()
+        st = wrecv0[:, :, 512:640].astype(F32).reshape(C_DEV * OWN, 128)
         m = (st + pltpu.roll(st, 96, 1)) + pltpu.roll(st, 64, 1)
         den = pltpu.roll(st, 32, 1)
         m3 = m.reshape(C_DEV, OWN, 128)
@@ -364,9 +373,17 @@
         fac = (fac / whole[None]).reshape(C_DEV * OWN, 128)
         high = fac.astype(BF16)
         low = (fac - high.astype(F32)).astype(BF16)
-        wide = nn(jnp.concatenate([high, low], axis=1), expand_v[...]).reshape(C_DEV, OWN, D)
-        attended = jnp.sum(wide * wrecv[:, :, 0:D].astype(F32), axis=0).astype(BF16)
-        seq_new = (resid + nn(attended, wout_v[...])).astype(BF16).astype(F32)
+        fac2_v[...] = jnp.concatenate([high, low], axis=1)
+        update = resid
+        for g in range(2):
+            land = (wrecv0, wrecv1)[g]
+            half = slice(g * 512, (g + 1) * 512)
+            if g == 1:
+                pltpu.make_async_copy(wrecv1, wrecv1, w1_recv).wait()
+            wide = nn(fac2_v[...], expand_v[:, half]).reshape(C_DEV, OWN, 512)
+            attended = jnp.sum(wide * land[:, :, 0:512].astype(F32), axis=0).astype(BF16)
+            update = update + nn(attended, wout_v[half, :])
+        seq_new = update.astype(BF16).astype(F32)
         proj = nn(wide_norm(seq_new).astype(BF16), wproj_v[...]).astype(BF16).astype(F32)
         turned = pltpu.roll(proj, 64, 1)
         lane8 = iota((OWN, 128), 1)
@@ -412,7 +429,8 @@
     def sent_rows(i, _):
         @pl.when(col_of(block_y(lax.div(i, 6)), lax.rem(i, 6)) != me_c)
         def _():
-            pltpu.make_async_copy(wmsg.at[i], wmsg.at[i], w_send).wait()
+            pltpu.make_async_copy(wmsg0.at[i], wmsg0.at[i], w0_send).wait()
+            pltpu.make_async_copy(wmsg1.at[i], wmsg1.at[i], w1_send).wait()
 
         return 0
 
@@ -529,15 +547,18 @@
             pltpu.VMEM((2, 16 * NJ, 512), BF16),
             pltpu.VMEM((2, NI, 16 * NJ), BF16),
             pltpu.VMEM((256, D), BF16),
-            pltpu.VMEM((OWNERS, OWN, WL), BF16),
-            pltpu.VMEM((C_DEV, OWN, WL), BF16),
+            pltpu.VMEM((C_DEV * OWN, 256), BF16),
+            pltpu.VMEM((OWNERS, OWN, 640), BF16),
+            pltpu.VMEM((OWNERS, OWN, 512), BF16),
+            pltpu.VMEM((C_DEV, OWN, 640), BF16),
+            pltpu.VMEM((C_DEV, OWN, 512), BF16),
             pltpu.VMEM((C_DEV, OWN, 128), BF16),
             pltpu.VMEM((OWNERS, OWN, 128), BF16),
             pltpu.VMEM((OWN, 128), BF16),
             pltpu.VMEM((6, OWN, 128), BF16),
             dma((9,)),
             dma((STEPS,)),
-            dma, dma, dma, dma, dma, dma, dma, dma, dma, dma, dma,
+            dma, dma, dma, dma, dma, dma, dma, dma, dma, dma, dma, dma, dma,
         ],
         compiler_params=pltpu.CompilerParams(
             collective_id=0, has_side_effects=True, vmem_limit_bytes=60 * 1024 * 1024

time: 43.4 us -> 42.8 us (0.986); the launches traced: 42.7 us -> 42.7 us
  no operation moved by 1% of the time
where the time goes in v5:
time: 42.8 us; the launch traced here: 42.7 us
  Pallas kernels  42.1 us (98%)
  between operations  0.64 us (1%)
    pallas_call x1, Pallas kernels, local(): pl.pallas_call(main_kernel, out_shape=(jax.ShapeDtypeStruct((NI, NJ, C),...  38.4 us
    pallas_call x1, Pallas kernels, local(): pl.pallas_call(pair_kernel, out_shape=(jax.ShapeDtypeStruct((NI, NJ, C),...  3.63 us

profile of v5, /device:TPU:1, one launch (start us, length us, event | category | flops | bytes accessed | tf_op | source)
XLA Modules:
  0.0 42.7 jit_solution(4735985874071054072)
XLA Ops:
  0.6 38.4 %trunk_main.1 = (bf16[192,48,128]{2,1,0:T(8,128)(2,1)}, bf16[24,8,128]{2,1,0:T(8,128)(2,1)}, bf16[6,8,128]{2,1,0:T(8,128)(2,1)}) custom-call(bf16[192,48,128]{2,1,0:T(8,128)(2,1)} %pair_h.1, bf16[32,1536]{1,0:T(8,128)(2,1)} %bitcast.3, bf16[128,512]{1,0:T(8,128)(2,1)} %whid_h.1, bf16[512,128]{1,0:T(8,128)(2,1)} %wback_h.1, bf16[32,128]{1,0:T(8,128)(2,1)} %bitcast.4, ...), custom_call_target="tpu_custom_call" | custom-call | tf_op jit(solution)/shard_map/trunk_main/pallas_call | solution.py:508
  39.1 3.6 %pair_update.1 = (bf16[192,48,128]{2,1,0:T(8,128)(2,1)}, bf16[32,192]{1,0:T(8,128)(2,1)}) custom-call(bf16[192,48,128]{2,1,0:T(8,128)(2,1)} %get-tuple-element.7.mid_h, bf16[24,8,128]{2,1,0:T(8,128)(2,1)} %get-tuple-element.8.left_h, bf16[6,8,128]{2,1,0:T(8,128)(2,1)} %get-tuple-element.9.right_h, bf16[128,128]{1,0:T(8,128)(2,1)} %wpair_h.1), custom_call_target="tpu_custom_call" | custom-call | tf_op jit(solution)/shard_map/pair_update/pallas_call | solution.py:568

commit v6 on v5

--- a/solution.py
+++ b/solution.py
@@ -389,25 +389,25 @@
         lane8 = iota((OWN, 128), 1)
         right = jnp.where(lane8 < 64, turned, proj).astype(BF16)
         rmsg[...] = right
+        slot = lax.rem(own_o, 6)
+        for r in range(R_DEV):
+            here = jnp.logical_and(r == me_r, dest_c == me_c)
+
+            @pl.when(jnp.logical_not(here))
+            def _():
+                pltpu.make_async_remote_copy(
+                    rmsg, rrecv.at[slot], r_send, r_recv, device_id=(r, dest_c), device_id_type=MESH
+                ).start()
+
+            @pl.when(here)
+            def _():
+                pltpu.make_async_copy(rmsg, rrecv.at[slot], r_recv).start()
+
         for c in range(C_DEV):
             tile = seq_new[:, (c // 4) * 128 : (c // 4) * 128 + 128]
             if c % 4 != 2:
                 tile = pltpu.roll(tile, (192 - 32 * (c % 4)) % 128, 1)
             emsg[c] = jnp.where(lane8 < 64, proj, tile).astype(BF16)
-
-        slot = lax.rem(own_o, 6)
-        for r in range(R_DEV):
-            here = jnp.logical_and(r == me_r, dest_c == me_c)
-
-            @pl.when(jnp.logical_not(here))
-            def _():
-                pltpu.make_async_remote_copy(
-                    rmsg, rrecv.at[slot], r_send, r_recv, device_id=(r, dest_c), device_id_type=MESH
-                ).start()
-
-            @pl.when(here)
-            def _():
-                pltpu.make_async_copy(rmsg, rrecv.at[slot], r_recv).start()
 
         for s in range(1, C_DEV):
             dst = lax.rem(me_c + (s + 15) % 31 + 1, C_DEV)

time: 42.8 us -> 42.8 us (level)
  no operation moved by 1% of the time
where the time goes in v6:
time: 42.8 us; the launch traced here: 42.7 us
  Pallas kernels  42.1 us (98%)
  between operations  0.64 us (1%)
    pallas_call x1, Pallas kernels, local(): pl.pallas_call(main_kernel, out_shape=(jax.ShapeDtypeStruct((NI, NJ, C),...  38.4 us
    pallas_call x1, Pallas kernels, local(): pl.pallas_call(pair_kernel, out_shape=(jax.ShapeDtypeStruct((NI, NJ, C),...  3.64 us

profile of v6, /device:TPU:1, one launch (start us, length us, event | category | flops | bytes accessed | tf_op | source)
XLA Modules:
  0.0 42.7 jit_solution(14320864523155169575)
XLA Ops:
  0.6 38.4 %trunk_main.1 = (bf16[192,48,128]{2,1,0:T(8,128)(2,1)}, bf16[24,8,128]{2,1,0:T(8,128)(2,1)}, bf16[6,8,128]{2,1,0:T(8,128)(2,1)}) custom-call(bf16[192,48,128]{2,1,0:T(8,128)(2,1)} %pair_h.1, bf16[32,1536]{1,0:T(8,128)(2,1)} %bitcast.3, bf16[128,512]{1,0:T(8,128)(2,1)} %whid_h.1, bf16[512,128]{1,0:T(8,128)(2,1)} %wback_h.1, bf16[32,128]{1,0:T(8,128)(2,1)} %bitcast.4, ...), custom_call_target="tpu_custom_call" | custom-call | tf_op jit(solution)/shard_map/trunk_main/pallas_call | solution.py:508
  39.1 3.6 %pair_update.1 = (bf16[192,48,128]{2,1,0:T(8,128)(2,1)}, bf16[32,192]{1,0:T(8,128)(2,1)}) custom-call(bf16[192,48,128]{2,1,0:T(8,128)(2,1)} %get-tuple-element.7.mid_h, bf16[24,8,128]{2,1,0:T(8,128)(2,1)} %get-tuple-element.8.left_h, bf16[6,8,128]{2,1,0:T(8,128)(2,1)} %get-tuple-element.9.right_h, bf16[128,128]{1,0:T(8,128)(2,1)} %wpair_h.1), custom_call_target="tpu_custom_call" | custom-call | tf_op jit(solution)/shard_map/pair_update/pallas_call | solution.py:568
